TPU v7x, 32 devices: a whole 2x2x4 slice. The times are simulated.
32 devices in a mesh: agent: 8 (over y, x, core), res: 4 (over z).
Axes of the slice: x: 2, y: 2, z: 4, core: 2. Of those that a mesh axis runs over, the one named last changes fastest.
Arguments:
- linear_cost: float32 [2048, 2048], P('agent', 'res'), may hold values from -6 to 6
- agent_type: int32 [2048], P('agent'), may hold values from 0 to 3, as said below
- block_mask: int32 [2048, 16], P('agent', 'res'), may hold values 0 or 1
- inverses: bfloat16 [4, 2048, 2048], P(None, 'res'), as said below
- cost_weight: float32 [2048], P('res'), may hold values from 0.5 to 8
- target: float32 [2048], P('res'), may hold values from -6 to 6
Outputs:
- usage: float32 [2048, 2048], P('agent', 'res')
- shared: float32 [2048], P('res')
- prices: float32 [2048], P('res')
- primal_norm: float32 [5], replicated
- dual_norm: float32 [5], replicated
Inputs may be any that keep to these rules, and one draw needn't show every extreme that they name: Each inverses[k] is exactly symmetric: inverses[k, i, j] equals inverses[k, j, i]. `agent_type`: each aligned block of 256 agents (the agents held by one device along the agent axis) holds exactly 64 agents of each type, in no particular order.
All inputs are finite; a program needn't handle non-finite values. No bound on the sum of `block_mask` on one device may be relied on, other than what follows from the above.
Results may differ from a plain program's by a relative error of at most 0.0039.
Values may be sent and summed in bfloat16 or wider, within the bound.
No kernel may reach another device: no remote copies, remote signals or barrier semaphores. Data moves between devices by JAX's collectives and lax.ppermute only.
A program may use at most 64 MiB of HBM per device.

v0:
```python
import jax
import jax.numpy as jnp
from jax import lax
from jax.sharding import PartitionSpec as P

BLK = 128
ITERS = 5


penalty = 1.0
eps = 1e-06


def on_device(linear_cost, agent_type, block_mask, inverses, cost_weight, target):
    local_agents, local_width = linear_cost.shape
    type_count = inverses.shape[0]
    group_rows = local_agents // type_count
    count = local_agents * lax.axis_size("agent")
    block_count = block_mask.shape[1]
    order = jnp.argsort(agent_type, stable=True)
    restore = jnp.argsort(order, stable=True)
    expand = jnp.broadcast_to(
        block_mask.astype(jnp.float32)[:, :, None], (local_agents, block_count, BLK)
    ).reshape(local_agents, local_width)
    usage = jnp.zeros(linear_cost.shape, jnp.float32)
    mean_usage = jnp.zeros((local_width,), jnp.float32)
    shared = jnp.zeros((local_width,), jnp.float32)
    prices = jnp.zeros((local_width,), jnp.float32)
    primal_list = []
    dual_list = []
    for iteration in range(ITERS):
        rhs = (penalty * (usage - mean_usage + shared - prices) - linear_cost).astype(jnp.bfloat16)
        grouped = rhs[order].reshape(type_count, group_rows, local_width)
        product = jnp.einsum(
            "tas,tws->taw",
            lax.all_gather(grouped, "res", axis=2, tiled=True),
            inverses,
            preferred_element_type=jnp.float32,
        )
        new_usage = product.reshape(local_agents, local_width)[restore]
        new_usage = new_usage * expand
        change_local = penalty * penalty * jnp.sum((new_usage - usage) ** 2)
        usage = new_usage
        column_sum = jnp.sum(usage, axis=0)
        usage_sum = lax.psum(column_sum, "agent")
        dual2 = lax.psum(change_local, ("agent", "res"))
        mean_usage = usage_sum / count
        shared = (cost_weight * target + penalty * (prices + mean_usage)) / (cost_weight + penalty)
        prices = prices + mean_usage - shared
        primal2 = lax.psum(count * jnp.sum((mean_usage - shared) ** 2), "res")
        primal_list.append(jnp.sqrt(primal2 + eps))
        dual_list.append(jnp.sqrt(dual2 + eps))
    primal_norm = jnp.stack(primal_list)
    dual_norm = jnp.stack(dual_list)
    return (usage, shared, prices, primal_norm, dual_norm)


def solution(mesh):
    placed = (
        P("agent", "res"),
        P("agent"),
        P("agent", "res"),
        P(None, "res", None),
        P("res"),
        P("res"),
    )
    return jax.shard_map(
        on_device,
        mesh=mesh,
        in_specs=placed,
        out_specs=(P("agent", "res"), P("res"), P("res"), P(), P()),
        check_vma=False,
    )
```

profile of v0, /device:TPU:0, one launch (start us, length us, event | category | flops | bytes accessed | tf_op | source)
XLA Modules:
  0.0 334.6 jit_solution(6932095263842248031)
XLA Ops:
  7.2 3.8 %sort.31 = (s32[256]{0:T(256)}, s32[256]{0:T(256)S(1)}) sort(s32[256]{0:T(256)} %param.7, s32[256]{0:T(256)S(1)} %iota.7), dimensions={0}, to_apply=%region_0.0 | sort | flops 2048 | bytes 4096 | tf_op jit(solution)/shard_map/jit(argsort)/sort | solution.py:20
  11.1 1.1 subtract_convert_fusion.4
  12.2 1.9 gather_fusion
  14.1 3.2 sort.32
  18.2 26.8 %all-gather.6.cloned.1.call-done = bf16[4,64,2048]{2,1,0:T(8,128)(2,1)} async-done(((bf16[4,64,512]{2,1,0:T(8,128)(2,1)}), bf16[4,64,2048]{2,1,0:T(8,128)(2,1)}) %all-gather.6.cloned.1.call-update) | async-done | bytes 1048592 | tf_op jit(solution)/shard_map/all_gather | solution.py:36
  45.0 6.4 %fusion.13 = f32[4,64,512]{2,1,0:T(8,128)S(1)} fusion(bf16[4,64,2048]{2,1,0:T(8,128)(2,1)} %all-gather.6.cloned.1.call-done, bf16[4,512,2048]{2,1,0:T(8,128)(2,1)} %param.9), kind=kOutput, calls=%fused_computation.56 | convolution fusion | flops 536870912 | bytes 9961472 | tf_op jit(solution)/shard_map/tas,tws->taw/dot_general | solution.py:34
  51.3 1.0 gather_fusion.1
  52.8 13.1 %psum.105 = f32[512]{0:T(512)S(1)} all-reduce(f32[512]{0:T(512)S(1)} %get-tuple-element.44), channel_id=1, replica_groups=mesh['agent'=8,'res'=4] {'agent'}, use_global_device_ids=true, to_apply=%region_3.4 | all-reduce | flops 512 | bytes 4096 | tf_op jit(solution)/shard_map/psum | solution.py:45
  66.6 1.9 gather_fusion.2
  68.5 26.2 %all-gather.8.cloned.1.call-done = bf16[4,64,2048]{2,1,0:T(8,128)(2,1)} async-done(((bf16[4,64,512]{2,1,0:T(8,128)(2,1)}), bf16[4,64,2048]{2,1,0:T(8,128)(2,1)}) %all-gather.8.cloned.1.call-update) | async-done | bytes 1048592 | tf_op jit(solution)/shard_map/all_gather | solution.py:36
  94.8 6.4 %fusion.14 = f32[4,64,512]{2,1,0:T(8,128)S(1)} fusion(bf16[4,64,2048]{2,1,0:T(8,128)(2,1)} %all-gather.8.cloned.1.call-done, bf16[4,512,2048]{2,1,0:T(8,128)(2,1)} %param.9), kind=kOutput, calls=%fused_computation.57 | convolution fusion | flops 536870912 | bytes 9961472 | tf_op jit(solution)/shard_map/tas,tws->taw/dot_general | solution.py:34
  101.1 1.0 gather_fusion.3
  102.2 13.1 %psum.106 = f32[512]{0:T(512)S(1)} all-reduce(f32[512]{0:T(512)S(1)} %get-tuple-element.42), channel_id=1, replica_groups=mesh['agent'=8,'res'=4] {'agent'}, use_global_device_ids=true, to_apply=%region_5.6 | all-reduce | flops 512 | bytes 4096 | tf_op jit(solution)/shard_map/psum | solution.py:45
  116.1 1.9 gather_fusion.4
  118.0 26.2 %all-gather.10.cloned.1.call-done = bf16[4,64,2048]{2,1,0:T(8,128)(2,1)} async-done(((bf16[4,64,512]{2,1,0:T(8,128)(2,1)}), bf16[4,64,2048]{2,1,0:T(8,128)(2,1)}) %all-gather.10.cloned.1.call-update) | async-done | bytes 1048592 | tf_op jit(solution)/shard_map/all_gather | solution.py:36
  144.2 6.4 %fusion.15 = f32[4,64,512]{2,1,0:T(8,128)S(1)} fusion(bf16[4,64,2048]{2,1,0:T(8,128)(2,1)} %all-gather.10.cloned.1.call-done, bf16[4,512,2048]{2,1,0:T(8,128)(2,1)} %param.9), kind=kOutput, calls=%fused_computation.58 | convolution fusion | flops 536870912 | bytes 9961472 | tf_op jit(solution)/shard_map/tas,tws->taw/dot_general | solution.py:34
  150.6 1.0 gather_fusion.5
  151.7 13.3 %psum.107 = f32[512]{0:T(512)S(1)} all-reduce(f32[512]{0:T(512)S(1)} %get-tuple-element.40), channel_id=1, replica_groups=mesh['agent'=8,'res'=4] {'agent'}, use_global_device_ids=true, to_apply=%region_7.8 | all-reduce | flops 512 | bytes 4096 | tf_op jit(solution)/shard_map/psum | solution.py:45
  165.7 1.9 gather_fusion.6
  167.7 26.2 %all-gather.12.cloned.1.call-done = bf16[4,64,2048]{2,1,0:T(8,128)(2,1)} async-done(((bf16[4,64,512]{2,1,0:T(8,128)(2,1)}), bf16[4,64,2048]{2,1,0:T(8,128)(2,1)}) %all-gather.12.cloned.1.call-update) | async-done | bytes 1048592 | tf_op jit(solution)/shard_map/all_gather | solution.py:36
  193.9 6.4 %fusion.16 = f32[4,64,512]{2,1,0:T(8,128)S(1)} fusion(bf16[4,64,2048]{2,1,0:T(8,128)(2,1)} %all-gather.12.cloned.1.call-done, bf16[4,512,2048]{2,1,0:T(8,128)(2,1)} %param.9), kind=kOutput, calls=%fused_computation.59 | convolution fusion | flops 536870912 | bytes 9961472 | tf_op jit(solution)/shard_map/tas,tws->taw/dot_general | solution.py:34
  200.3 1.8 gather_fusion.7
  202.0 1.2 fusion.9
  203.2 13.1 %psum.108 = f32[512]{0:T(512)S(1)} all-reduce(f32[512]{0:T(512)S(1)} %get-tuple-element.38), channel_id=1, replica_groups=mesh['agent'=8,'res'=4] {'agent'}, use_global_device_ids=true, to_apply=%region_9.10 | all-reduce | flops 512 | bytes 4096 | tf_op jit(solution)/shard_map/psum | solution.py:45
  217.0 1.9 gather_fusion.8
  221.5 23.7 %all-gather.14.cloned.1.call-done = bf16[4,64,2048]{2,1,0:T(8,128)(2,1)} async-done(((bf16[4,64,512]{2,1,0:T(8,128)(2,1)}), bf16[4,64,2048]{2,1,0:T(8,128)(2,1)}) %all-gather.14.cloned.1.call-update) | async-done | bytes 1048592 | tf_op jit(solution)/shard_map/all_gather | solution.py:36
  245.2 6.4 %fusion.17 = f32[4,64,512]{2,1,0:T(8,128)S(1)} fusion(bf16[4,64,2048]{2,1,0:T(8,128)(2,1)} %all-gather.14.cloned.1.call-done, bf16[4,512,2048]{2,1,0:T(8,128)(2,1)} %param.9), kind=kOutput, calls=%fused_computation.60 | convolution fusion | flops 536870912 | bytes 9961472 | tf_op jit(solution)/shard_map/tas,tws->taw/dot_general | solution.py:34
  251.5 1.8 gather_fusion.9
  253.3 2.8 multiply_reduce_fusion
  256.1 13.1 %psum.109 = f32[512]{0:T(512)S(1)} all-reduce(f32[512]{0:T(512)S(1)} %get-tuple-element.14), channel_id=1, replica_groups=mesh['agent'=8,'res'=4] {'agent'}, use_global_device_ids=true, to_apply=%region_11.12 | all-reduce | flops 512 | bytes 4096 | tf_op jit(solution)/shard_map/psum | solution.py:45
  271.1 11.3 %all-reduce.1 = (f32[]{:T(128)}, f32[]{:T(128)}, f32[]{:T(128)}, f32[]{:T(128)}, f32[]{:T(128)}) all-reduce(f32[]{:T(128)S(6)} %mul.99, f32[]{:T(128)S(6)} %mul.100, f32[]{:T(128)S(6)} %mul.101, f32[]{:T(128)S(6)} %mul.102, f32[]{:T(128)S(6)} %mul.103), channel_id=1, replica_groups=mesh['agent'=8,'res'=4] {'res'}, use_global_device_ids=true, to_apply=%region_13.14 | all-reduce | flops 5 | bytes 40 | tf_op jit(solution)/shard_map/psum | solution.py:50
  285.7 37.7 %all-reduce = (f32[]{:T(128)}, f32[]{:T(128)}, f32[]{:T(128)}, f32[]{:T(128)}, f32[]{:T(128)}) all-reduce(f32[]{:T(128)} %get-tuple-element.13, f32[]{:T(128)} %get-tuple-element.12, f32[]{:T(128)} %get-tuple-element.11, f32[]{:T(128)} %get-tuple-element.10, f32[]{:T(128)} %get-tuple-element.9), channel_id=1, replica_groups=mesh['agent'=8,'res'=4] {'agent','res'}, use_global_device_ids=true, to_apply=%region_23.24 | all-reduce | flops 5 | bytes 40 | tf_op jit(solution)/shard_map/psum | solution.py:46
  (45 shorter events, 7.2 us)
Async XLA Ops:
  7.2 37.8 %all-gather.6.cloned.1.call-start = ((), (), s32[]{:S(2)}) async-start(), calls=%async_computation | async-start | bytes 1310720 | tf_op jit(solution)/shard_map/all_gather | solution.py:36
  14.0 80.7 %all-gather.8.cloned.1.call-start = ((), (), s32[]{:S(2)}) async-start(), calls=%async_computation.1 | async-start | bytes 1310720 | tf_op jit(solution)/shard_map/all_gather | solution.py:36
  18.1 47.8 %copy-start.1 = (f32[512]{0:T(512)S(1)}, f32[512]{0:T(512)}, u32[]{:S(2)}) copy-start(f32[512]{0:T(512)} %param.10) | copy-start | bytes 6148
  18.1 47.8 %copy-start.3 = (f32[512]{0:T(512)S(1)}, f32[512]{0:T(512)}, u32[]{:S(2)}) copy-start(f32[512]{0:T(512)} %param.11) | copy-start | bytes 6148
  18.1 48.4 %copy-start = (f32[256,512]{1,0:T(8,128)S(1)}, f32[256,512]{1,0:T(8,128)}, u32[]{:S(2)}) copy-start(f32[256,512]{1,0:T(8,128)} %param.6) | copy-start | bytes 1572868
  68.5 75.7 %all-gather.10.cloned.1.call-start = ((), (), s32[]{:S(2)}) async-start(), calls=%async_computation.2 | async-start | bytes 1310720 | tf_op jit(solution)/shard_map/all_gather | solution.py:36
  118.0 75.9 %all-gather.12.cloned.1.call-start = ((), (), s32[]{:S(2)}) async-start(), calls=%async_computation.3 | async-start | bytes 1310720 | tf_op jit(solution)/shard_map/all_gather | solution.py:36
  167.6 77.6 %all-gather.14.cloned.1.call-start = ((), (), s32[]{:S(2)}) async-start(), calls=%async_computation.4 | async-start | bytes 1310720 | tf_op jit(solution)/shard_map/all_gather | solution.py:36
  269.9 58.2 %copy-start.2 = (f32[512]{0:T(512)}, f32[512]{0:T(512)S(1)}, u32[]{:S(2)}) copy-start(f32[512]{0:T(512)S(1)} %get-tuple-element.26) | copy-start | bytes 6148
Sparse Core Ops, SparseCore 0:
  14.2 30.7 all-gather.5
  68.6 26.0 all-gather.7
  118.1 26.0 all-gather.9
  167.7 26.0 all-gather.11
  219.0 26.0 all-gather.13
where the time goes:
time: 336 us; the launch traced here: 335 us
  waiting for transfers between devices  129 us (38%)
  blocking collectives  115 us (34%)
  matrix products  31.9 us (9%)
  between operations  23.8 us (7%)
  local copies, waits for them, and re-layouts  17.4 us (5%)
  other arithmetic  17.3 us (5%)
    all_gather x5, waiting for transfers between devices, on_device(): lax.all_gather(grouped, 'res', axis=2, tiled=True)  129 us
    psum x5, blocking collectives, on_device(): usage_sum = lax.psum(column_sum, 'agent')  65.8 us
    psum x1, blocking collectives, on_device(): dual2 = lax.psum(change_local, ('agent', 'res'))  37.7 us
    dot_general x5, matrix products, on_device(): jnp.einsum('tas,tws->taw', lax.all_gather(grouped, 'res', axis=2, tiled=T...  31.9 us
    psum x1, blocking collectives, on_device(): primal2 = lax.psum(count * jnp.sum((mean_usage - shared) ** 2), 'res')  11.3 us
    gather x5, local copies, waits for them, and re-layouts, on_device(): grouped = rhs[order].reshape(type_count, group_rows, local_width)  9.27 us
  transfers between devices with their start and end apart: 5, of which 5 were waited for; matrix products, arithmetic and copies ran while one was open for 1% of the time, Pallas kernels for 0%

commit v1 on v0

v1 whole, which is shorter than its diff:
```python
import functools

import jax
import jax.numpy as jnp
from jax import lax
from jax.experimental import pallas as pl
from jax.experimental.pallas import tpu as pltpu
from jax.sharding import PartitionSpec as P

ITERS = 5
LANES = 128

penalty = 1.0
eps = 1e-06

VMEM = pl.BlockSpec(memory_space=pltpu.VMEM)
SMEM = pl.BlockSpec(memory_space=pltpu.SMEM)
F32 = jnp.float32
BF16 = jnp.bfloat16


def call(body, out_shape, args, scalars=0, name=None, flops=0, limit=24 << 20, scratch=()):
    moved = sum(a.size * a.dtype.itemsize for a in args)
    return pl.pallas_call(
        body,
        out_shape=out_shape,
        in_specs=[SMEM] * scalars + [VMEM] * (len(args) - scalars),
        out_specs=jax.tree.map(lambda _: VMEM, out_shape),
        scratch_shapes=scratch,
        compiler_params=pltpu.CompilerParams(vmem_limit_bytes=limit),
        cost_estimate=pl.CostEstimate(flops=flops, bytes_accessed=moved, transcendentals=0),
        name=name,
    )(*args)


def shaped(shape, dtype):
    return jax.ShapeDtypeStruct(shape, dtype)


def split(value):
    high = value.astype(BF16)
    return high, (value - high.astype(F32)).astype(BF16)


def three(value):
    high = value.astype(BF16)
    rest = value - high.astype(F32)
    middle = rest.astype(BF16)
    return high, middle, (rest - middle.astype(F32)).astype(BF16)


def prep_kernel(types, cost_ref, kind_ref, mask_ref, high_ref, low_ref, expand_ref, sort_ref):
    agents, width = cost_ref.shape
    blocks = mask_ref.shape[1]
    kind = kind_ref[...]
    row = lax.broadcasted_iota(jnp.int32, (agents, agents), 0)
    column = lax.broadcasted_iota(jnp.int32, (agents, agents), 1)
    earlier = (row < column).astype(F32).astype(BF16)
    type_of = lax.broadcasted_iota(jnp.int32, (16, agents), 0)
    member = (jnp.broadcast_to(kind, (16, agents)) == type_of).astype(F32)
    rank = jnp.dot(member.astype(BF16), earlier, preferred_element_type=F32)
    start = type_of.astype(F32) * (agents // types)
    place = jnp.sum(member * (rank + start), axis=0, keepdims=True)
    sort = (row.astype(F32) == jnp.broadcast_to(place, (agents, agents))).astype(F32).astype(BF16)
    sort_ref[...] = sort
    high, low = split(-cost_ref[...])
    high_ref[...] = jnp.dot(sort, high, preferred_element_type=F32).astype(BF16)
    low_ref[...] = jnp.dot(sort, low, preferred_element_type=F32).astype(BF16)
    mask = jnp.dot(sort, mask_ref[...].astype(F32).astype(BF16), preferred_element_type=F32)
    each = width // blocks
    for block in range(blocks):
        expand_ref[:, block * each:(block + 1) * each] = jnp.broadcast_to(
            mask[:, block:block + 1], (agents, each)
        )


def times(left, m_ref, kind, block):
    width = m_ref.shape[1]
    right = m_ref[kind, :, pl.ds(pl.multiple_of(block * width, LANES), width)]
    return lax.dot_general(left, right, (((1,), (1,)), ((), ())), preferred_element_type=F32)


def first_kernel(slots, me_ref, *refs):
    low_ref, m_ref, acc_ref = refs[slots], refs[slots + 1], refs[slots + 2]
    types = m_ref.shape[0]
    group = low_ref.shape[0] // types
    me = me_ref[0]
    for kind in range(types):
        rows = slice(kind * group, (kind + 1) * group)
        both = jnp.concatenate([refs[0][rows], low_ref[rows]], axis=0)
        own = times(both, m_ref, kind, me)
        total = own[:group] + own[group:]
        for slot in range(1, slots):
            total += times(refs[slot][rows], m_ref, kind, me ^ slot)
        acc_ref[rows] = total


def vectors(received_ref, weight, target, prices, per_block, count):
    width = weight.shape[1]
    parts, changes = [], []
    blocks = weight.shape[0]
    for block in range(blocks):
        rows = received_ref[block * per_block:(block + 1) * per_block]
        parts.append(jnp.sum(rows[:, :width], axis=0, keepdims=True))
        changes.append(jnp.sum(rows[:, width:], axis=0, keepdims=True))
    mean = jnp.concatenate(parts, axis=0) / count
    shared = (weight * target + penalty * (prices + mean)) / (weight + penalty)
    prices = prices + mean - shared
    gap = mean - shared
    primal = count * jnp.sum(gap * gap)
    dual = penalty * penalty * jnp.sum(sum(changes))
    return mean, shared, prices, primal, dual


def norms_of(norms, step, primal, dual):
    lane = lax.broadcasted_iota(jnp.int32, norms.shape, 1)
    row = lax.broadcasted_iota(jnp.int32, norms.shape, 0)
    norms = jnp.where((lane == step) & (row == 0), jnp.sqrt(primal + eps), norms)
    return jnp.where((lane == step) & (row == 1), jnp.sqrt(dual + eps), norms)


def mid_kernel(slots, step, per_block, count, me_ref, *refs):
    usage_ref, received_ref, weight_ref, target_ref, prices_ref, norms_ref, base_ref, m_ref = refs[slots:slots + 8]
    acc_ref, new_prices_ref, new_norms_ref, v_ref = refs[slots + 8:]
    types, width = m_ref.shape[:2]
    blocks = m_ref.shape[2] // width
    group = base_ref.shape[0] // types
    me = me_ref[0]
    mean, shared, prices, primal, dual = vectors(
        received_ref, weight_ref[...], target_ref[...], prices_ref[...], per_block, count
    )
    new_prices_ref[...] = prices
    new_norms_ref[...] = norms_of(norms_ref[...], step, primal, dual)
    v_ref[...] = shared - mean - prices
    row = lax.broadcasted_iota(jnp.int32, (16, width), 0)
    lefts = []
    for slot in range(blocks):
        value = v_ref[pl.ds(me ^ slot, 1), :]
        high, middle, low = (jnp.broadcast_to(x.astype(F32), (16, width)) for x in three(value))
        lefts.append(
            jnp.where(row == 0, high, jnp.where(row == 1, middle, jnp.where(row == 2, low, 0.0))).astype(BF16)
        )
    for kind in range(types):
        rows = slice(kind * group, (kind + 1) * group)
        own_high = refs[0][rows]
        own_low = (usage_ref[rows] - own_high.astype(F32)).astype(BF16)
        own = times(jnp.concatenate([own_high, own_low, lefts[0]], axis=0), m_ref, kind, me)
        total = own[:group] + own[group:2 * group]
        shift = own[2 * group:]
        for slot in range(1, blocks):
            if slot < slots:
                got = times(jnp.concatenate([refs[slot][rows], lefts[slot]], axis=0), m_ref, kind, me ^ slot)
                total += got[:group]
                shift += got[group:]
            else:
                shift += times(lefts[slot], m_ref, kind, me ^ slot)
        acc_ref[rows] = base_ref[rows] + total + jnp.sum(shift, axis=0, keepdims=True)


def late_kernel(first, me_ref, acc_ref, last_ref, expand_ref, usage_ref, m_ref, new_ref, sent_ref, payload_ref, *rest):
    types, width = m_ref.shape[:2]
    blocks = m_ref.shape[2] // width
    group = acc_ref.shape[0] // types
    me = me_ref[0]
    sums = jnp.zeros((8, width), F32)
    change = jnp.zeros((8, width), F32)
    for kind in range(types):
        rows = slice(kind * group, (kind + 1) * group)
        total = acc_ref[rows] + times(last_ref[rows], m_ref, kind, me ^ (blocks - 1))
        if first:
            rest[0][rows] = total
        new = expand_ref[rows] * total
        new_ref[rows] = new
        sent_ref[rows] = new.astype(BF16)
        moved = new if first else new - usage_ref[rows]
        sums += jnp.sum(new.reshape(group // 8, 8, width), axis=0)
        change += jnp.sum((moved * moved).reshape(group // 8, 8, width), axis=0)
    payload_ref[:, :width] = jnp.sum(sums, axis=0, keepdims=True)
    lanes = sum(change[:, at:at + LANES] for at in range(0, width, LANES))
    payload_ref[:, width:] = jnp.sum(lanes, axis=0, keepdims=True)


def last_kernel(step, per_block, count, me_ref, received_ref, weight_ref, target_ref, prices_ref, norms_ref,
                own_shared_ref, own_prices_ref, new_norms_ref, keep_ref):
    mean, shared, prices, primal, dual = vectors(
        received_ref, weight_ref[...], target_ref[...], prices_ref[...], per_block, count
    )
    new_norms_ref[...] = norms_of(norms_ref[...], step, primal, dual)
    keep_ref[...] = shared
    own_shared_ref[...] = keep_ref[pl.ds(me_ref[0], 1), :]
    keep_ref[...] = prices
    own_prices_ref[...] = keep_ref[pl.ds(me_ref[0], 1), :]


def restore_kernel(sort_ref, usage_ref, out_ref):
    total = None
    for piece in three(usage_ref[...]):
        got = lax.dot_general(sort_ref[...], piece, (((0,), (0,)), ((), ())), preferred_element_type=F32)
        total = got if total is None else total + got
    out_ref[...] = total


def on_device(linear_cost, agent_type, block_mask, inverses, cost_weight, target):
    agents, width = linear_cost.shape
    types = inverses.shape[0]
    per_block = lax.axis_size("agent")
    blocks = lax.axis_size("res")
    count = agents * per_block
    me = lax.axis_index("res").astype(jnp.int32).reshape(1)
    flops = 2 * agents * width * width

    def swap(value, bit):
        return lax.ppermute(value, "res", [(i, i ^ bit) for i in range(blocks)])

    def gather(own):
        slots = [own] + [None] * (blocks - 1)
        for slot in sorted(range(1, blocks), key=lambda m: (bin(m).count("1"), -m)):
            bit = slot & -slot
            slots[slot] = swap(slots[slot ^ bit], bit)
        return slots

    def spread(row):
        rows = jnp.broadcast_to(row, (blocks * per_block, row.shape[1]))
        return lax.all_to_all(rows, ("res", "agent"), 0, 0, tiled=True)

    high, low, expand, sort = call(
        functools.partial(prep_kernel, types),
        (shaped((agents, width), BF16), shaped((agents, width), BF16), shaped((agents, width), F32), shaped((agents, agents), BF16)),
        (linear_cost, agent_type.reshape(1, agents), block_mask),
        name="prep",
    )
    slots = gather(high)
    both = spread(jnp.concatenate([cost_weight, target]).reshape(1, 2 * width))[::per_block]
    weights, targets = both[:, :width], both[:, width:]
    prices = jnp.zeros((blocks, width), F32)
    norms = jnp.zeros((8, LANES), F32)
    base = usage = None
    for step in range(ITERS):
        if step == 0:
            acc = call(
                functools.partial(first_kernel, blocks - 1),
                shaped((agents, width), F32),
                (me, *slots[:-1], low, inverses),
                scalars=1, name="first", flops=flops * blocks,
            )
        else:
            acc, prices, norms = call(
                functools.partial(mid_kernel, blocks - 1, step - 1, per_block, count),
                (shaped((agents, width), F32), shaped((blocks, width), F32), shaped((8, LANES), F32)),
                (me, *slots[:-1], usage, received, weights, targets, prices, norms, base, inverses),
                scalars=1, name="mid", flops=flops * blocks,
                scratch=[pltpu.VMEM((blocks, width), F32)],
            )
        outs = (shaped((agents, width), F32), shaped((agents, width), BF16), shaped((1, width + LANES), F32))
        if step == 0:
            outs += (shaped((agents, width), F32),)
        got = call(
            functools.partial(late_kernel, step == 0),
            outs,
            (me, acc, slots[-1], expand, acc if usage is None else usage, inverses),
            scalars=1, name="late", flops=flops,
        )
        usage, sent, payload = got[:3]
        if step == 0:
            base = got[3]
        if step < ITERS - 1:
            slots = gather(sent)
        received = spread(payload)
    own_shared, own_prices, norms = call(
        functools.partial(last_kernel, ITERS - 1, per_block, count),
        (shaped((1, width), F32), shaped((1, width), F32), shaped((8, LANES), F32)),
        (me, received, weights, targets, prices, norms),
        scalars=1, name="last",
        scratch=[pltpu.VMEM((blocks, width), F32)],
    )
    out = call(restore_kernel, shaped((agents, width), F32), (sort, usage), name="restore")
    return out, own_shared.reshape(width), own_prices.reshape(width), norms[0, :ITERS], norms[1, :ITERS]


def solution(mesh):
    placed = (
        P("agent", "res"),
        P("agent"),
        P("agent", "res"),
        P(None, "res", None),
        P("res"),
        P("res"),
    )
    return jax.shard_map(
        on_device,
        mesh=mesh,
        in_specs=placed,
        out_specs=(P("agent", "res"), P("res"), P("res"), P(), P()),
        check_vma=False,
    )
```

time: 336 us -> 188 us (0.56)
  blocking collectives: 115 us -> 32.8 us
  waiting for transfers between devices: 129 us -> 71.6 us
  matrix products: 31.9 us -> 0 us
  starting transfers between devices: 0.21 us -> 28.4 us
  between operations: 23.8 us -> 0.94 us
  Pallas kernels: 0 us -> 20 us
  other arithmetic: 17.3 us -> 0.08 us
  local copies, waits for them, and re-layouts: 17.4 us -> 33.1 us
    all_gather x5 -> x0, waiting for transfers between devices: 129 us -> none  [on_device(): lax.all_gather(grouped, 'res', axis=2, tiled=True)]
    psum x7 -> x0, blocking collectives: 115 us -> none  [the longest x5 65.8 us: on_device(): usage_sum = lax.psum(column_sum, 'agent')]
    ppermute x0 -> x15, waiting for transfers between devices: none -> 49.2 us  [swap(): return lax.ppermute(value, 'res', [(i, i ^ bit) for i in range(blocks)])]
    all_to_all x0 -> x3, blocking collectives: none -> 32.8 us  [spread(): return lax.all_to_all(rows, ('res', 'agent'), 0, 0, tiled=True)]
    dot_general x5 -> x0, matrix products: 31.9 us -> none  [on_device(): jnp.einsum('tas,tws->taw', lax.all_gather(grouped, 'res', axis=2, tiled=T...]
    unnamed x8 -> x35, local copies, waits for them, and re-layouts: 0.02 us -> 30.3 us
    all_to_all x0 -> x3, waiting for transfers between devices: none -> 22.4 us  [spread(): return lax.all_to_all(rows, ('res', 'agent'), 0, 0, tiled=True)]
    pallas_call x0 -> x13, Pallas kernels: none -> 20 us  [call(): pl.pallas_call(body, out_shape=out_shape, in_specs=[SMEM] * scalars + [VM...]
  transfers between devices with their start and end apart: 5 -> 18, of which waited for: 5 -> 8; matrix products, arithmetic and copies ran while one was open for 1% -> 1% of each run, Pallas kernels for 0% -> 7%
where the time goes in v1:
time: 188 us; the launch traced here: 187 us
  waiting for transfers between devices  71.6 us (38%)
  local copies, waits for them, and re-layouts  33.1 us (18%)
  blocking collectives  32.8 us (17%)
  starting transfers between devices  28.4 us (15%)
  Pallas kernels  20 us (11%)
    ppermute x15, waiting for transfers between devices, swap(): return lax.ppermute(value, 'res', [(i, i ^ bit) for i in range(blocks)])  49.2 us
    all_to_all x3, blocking collectives, spread(): return lax.all_to_all(rows, ('res', 'agent'), 0, 0, tiled=True)  32.8 us
    unnamed x35, local copies, waits for them, and re-layouts  30.3 us
    all_to_all x3, waiting for transfers between devices, spread(): return lax.all_to_all(rows, ('res', 'agent'), 0, 0, tiled=True)  22.4 us
    pallas_call x13, Pallas kernels, call(): pl.pallas_call(body, out_shape=out_shape, in_specs=[SMEM] * scalars + [VM...  20 us
    ppermute x15, starting transfers between devices, swap(): return lax.ppermute(value, 'res', [(i, i ^ bit) for i in range(blocks)])  18.6 us
    all_to_all x3, starting transfers between devices, spread(): return lax.all_to_all(rows, ('res', 'agent'), 0, 0, tiled=True)  9.79 us
  transfers between devices with their start and end apart: 18, of which 8 were waited for; matrix products, arithmetic and copies ran while one was open for 1% of the time, Pallas kernels for 7%

profile of v1, /device:TPU:0, one launch (start us, length us, event | category | flops | bytes accessed | tf_op | source)
XLA Modules:
  0.0 186.9 jit_solution(11196511158552858048)
XLA Ops:
  3.9 4.1 %collective-permute-start.1 = (bf16[256,512]{1,0:T(8,128)(2,1)S(1)}, bf16[256,512]{1,0:T(8,128)(2,1)S(1)}, u32[]{:S(2)}, u32[]{:S(2)}) collective-permute-start(bf16[256,512]{1,0:T(8,128)(2,1)S(1)} %get-tuple-element.40.refs_0_), channel_id=1, source_target_pairs={{0,2},{1,3},{2,0},{3,1},{4,6},{5,7},{6,4},{7,5},{8,10},{9,11},{10,... | collective-permute-start | bytes 786440 | tf_op jit(solution)/shard_map/ppermute | solution.py:213
  8.0 1.6 collective-permute-start
  9.6 10.4 %collective-permute-done.1.refs_2_ = bf16[256,512]{1,0:T(8,128)(2,1)S(1)} collective-permute-done((bf16[256,512]{1,0:T(8,128)(2,1)S(1)}, bf16[256,512]{1,0:T(8,128)(2,1)S(1)}, u32[]{:S(2)}, u32[]{:S(2)}) %collective-permute-start.1) | collective-permute-done | bytes 262176 | tf_op jit(solution)/shard_map/ppermute | solution.py:213
  20.6 3.4 %copy-done = bf16[4,512,2048]{2,1,0:T(8,128)(2,1)S(1)} copy-done((bf16[4,512,2048]{2,1,0:T(8,128)(2,1)S(1)}, bf16[4,512,2048]{2,1,0:T(8,128)(2,1)}, u32[]{:S(2)}) %copy-start) | copy-done | bytes 8388632
  24.0 2.1 %first.1.acc_ref.usage_ref = f32[256,512]{1,0:T(8,128)S(1)} custom-call(s32[1]{0:T(128)} %bitcast.1.me_ref, bf16[256,512]{1,0:T(8,128)(2,1)S(1)} %get-tuple-element.40.refs_0_, bf16[256,512]{1,0:T(8,128)(2,1)S(1)} %collective-permute-done.refs_1_, bf16[256,512]{1,0:T(8,128)(2,1)S(1)} %collective-permute-done.1.refs_2_, ...), custom_call_target="tpu_custom_call" | custom-call | flops 536870912 | bytes 9437188 | tf_op jit(solution)/shard_map/first/pallas_call | solution.py:24
  28.2 3.4 %collective-permute-start.4 = (bf16[256,512]{1,0:T(8,128)(2,1)S(1)}, bf16[256,512]{1,0:T(8,128)(2,1)S(1)}, u32[]{:S(2)}, u32[]{:S(2)}) collective-permute-start(bf16[256,512]{1,0:T(8,128)(2,1)S(1)} %get-tuple-element.43.refs_0_), channel_id=1, source_target_pairs={{0,2},{1,3},{2,0},{3,1},{4,6},{5,7},{6,4},{7,5},{8,10},{9,11},{10,... | collective-permute-start | bytes 786440 | tf_op jit(solution)/shard_map/ppermute | solution.py:213
  32.4 3.7 %all-to-all-start.1 = ((f32[32,1,1024]{2,1,0:T(1,128)}), f32[32,1,1024]{2,1,0:T(1,128)S(1)}, u32[]{:S(2)}, u32[]{:S(2)}) async-start(f32[32,1,1024]{2,1,0:T(1,128)} %broadcast_in_dim.17), calls=%async_computation.1 | async-start | bytes 262144 | tf_op jit(solution)/shard_map/all_to_all | solution.py:224
  36.1 1.8 collective-permute-start.3
  38.0 10.0 %all-to-all-done.1 = f32[32,1,1024]{2,1,0:T(1,128)S(1)} async-done(((f32[32,1,1024]{2,1,0:T(1,128)}), f32[32,1,1024]{2,1,0:T(1,128)S(1)}, u32[]{:S(2)}, u32[]{:S(2)}) %all-to-all-start.1) | async-done | bytes 131104 | tf_op jit(solution)/shard_map/all_to_all | solution.py:224
  48.8 3.5 %all-to-all-start = ((f32[32,1,640]{2,1,0:T(1,128)}), f32[32,1,640]{2,1,0:T(1,128)S(1)}, u32[]{:S(2)}, u32[]{:S(2)}) async-start(f32[32,1,640]{2,1,0:T(1,128)} %broadcast_in_dim.16), calls=%async_computation | async-start | bytes 163840 | tf_op jit(solution)/shard_map/all_to_all | solution.py:224
  52.3 1.8 collective-permute-start.5
  54.1 6.0 %all-to-all-done = f32[32,1,640]{2,1,0:T(1,128)S(1)} async-done(((f32[32,1,640]{2,1,0:T(1,128)}), f32[32,1,640]{2,1,0:T(1,128)S(1)}, u32[]{:S(2)}, u32[]{:S(2)}) %all-to-all-start) | async-done | bytes 81952 | tf_op jit(solution)/shard_map/all_to_all | solution.py:224
  60.2 3.4 %copy-done.2 = bf16[4,512,2048]{2,1,0:T(8,128)(2,1)S(1)} copy-done((bf16[4,512,2048]{2,1,0:T(8,128)(2,1)S(1)}, bf16[4,512,2048]{2,1,0:T(8,128)(2,1)}, u32[]{:S(2)}) %copy-start.2) | copy-done | bytes 8388632
  63.6 2.7 %mid.4 = (f32[256,512]{1,0:T(8,128)S(1)}, f32[4,512]{1,0:T(4,128)S(1)}, f32[8,128]{1,0:T(8,128)S(1)}) custom-call(s32[1]{0:T(128)} %bitcast.1.me_ref, bf16[256,512]{1,0:T(8,128)(2,1)S(1)} %get-tuple-element.43.refs_0_, bf16[256,512]{1,0:T(8,128)(2,1)S(1)} %collective-permute-done.3.refs_1_, bf16[256,512]{1,0:T(8,128)(2,1)S(1)} %collective-permute-done.4.refs_2_, ...), custom_call_target="tpu_custom_call" | custom-call | flops 536870912 | bytes 10334212 | tf_op jit(solution)/shard_map/mid/pallas_call | solution.py:24
  69.1 12.8 %collective-permute-done.7.refs_2_ = bf16[256,512]{1,0:T(8,128)(2,1)S(1)} collective-permute-done((bf16[256,512]{1,0:T(8,128)(2,1)S(1)}, bf16[256,512]{1,0:T(8,128)(2,1)S(1)}, u32[]{:S(2)}, u32[]{:S(2)}) %collective-permute-start.7) | collective-permute-done | bytes 262176 | tf_op jit(solution)/shard_map/ppermute | solution.py:213
  82.0 10.6 %all_to_all.49 = f32[32,1,640]{2,1,0:T(1,128)S(1)} all-to-all(f32[32,1,640]{2,1,0:T(1,128)S(1)} %broadcast_in_dim.40), channel_id=1, replica_groups=mesh['agent'=8,'res'=4] {'res','agent'}, dimensions={0} | all-to-all | bytes 163840 | tf_op jit(solution)/shard_map/all_to_all | solution.py:224
  92.6 3.4 %copy-done.4 = bf16[4,512,2048]{2,1,0:T(8,128)(2,1)S(1)} copy-done((bf16[4,512,2048]{2,1,0:T(8,128)(2,1)S(1)}, bf16[4,512,2048]{2,1,0:T(8,128)(2,1)}, u32[]{:S(2)}) %copy-start.4) | copy-done | bytes 8388632
  96.0 2.7 %mid.5 = (f32[256,512]{1,0:T(8,128)S(1)}, f32[4,512]{1,0:T(4,128)S(1)}, f32[8,128]{1,0:T(8,128)S(1)}) custom-call(s32[1]{0:T(128)} %bitcast.1.me_ref, bf16[256,512]{1,0:T(8,128)(2,1)S(1)} %get-tuple-element.48.refs_0_, bf16[256,512]{1,0:T(8,128)(2,1)S(1)} %collective-permute-done.6.refs_1_, bf16[256,512]{1,0:T(8,128)(2,1)S(1)} %collective-permute-done.7.refs_2_, ...), custom_call_target="tpu_custom_call" | custom-call | flops 536870912 | bytes 10334212 | tf_op jit(solution)/shard_map/mid/pallas_call | solution.py:24
  98.7 3.4 %copy-done.5 = bf16[4,512,2048]{2,1,0:T(8,128)(2,1)S(1)} copy-done((bf16[4,512,2048]{2,1,0:T(8,128)(2,1)S(1)}, bf16[4,512,2048]{2,1,0:T(8,128)(2,1)}, u32[]{:S(2)}) %copy-start.5) | copy-done | bytes 8388632
  105.0 12.1 %collective-permute-done.10.refs_2_ = bf16[256,512]{1,0:T(8,128)(2,1)S(1)} collective-permute-done((bf16[256,512]{1,0:T(8,128)(2,1)S(1)}, bf16[256,512]{1,0:T(8,128)(2,1)S(1)}, u32[]{:S(2)}, u32[]{:S(2)}) %collective-permute-start.10) | collective-permute-done | bytes 262176 | tf_op jit(solution)/shard_map/ppermute | solution.py:213
  117.2 11.3 %all_to_all.50 = f32[32,1,640]{2,1,0:T(1,128)S(1)} all-to-all(f32[32,1,640]{2,1,0:T(1,128)S(1)} %broadcast_in_dim.41), channel_id=1, replica_groups=mesh['agent'=8,'res'=4] {'res','agent'}, dimensions={0} | all-to-all | bytes 163840 | tf_op jit(solution)/shard_map/all_to_all | solution.py:224
  128.5 3.4 %copy-done.6 = bf16[4,512,2048]{2,1,0:T(8,128)(2,1)S(1)} copy-done((bf16[4,512,2048]{2,1,0:T(8,128)(2,1)S(1)}, bf16[4,512,2048]{2,1,0:T(8,128)(2,1)}, u32[]{:S(2)}) %copy-start.6) | copy-done | bytes 8388632
  131.8 2.7 %mid.6 = (f32[256,512]{1,0:T(8,128)S(1)}, f32[4,512]{1,0:T(4,128)S(1)}, f32[8,128]{1,0:T(8,128)S(1)}) custom-call(s32[1]{0:T(128)} %bitcast.1.me_ref, bf16[256,512]{1,0:T(8,128)(2,1)S(1)} %get-tuple-element.54.refs_0_, bf16[256,512]{1,0:T(8,128)(2,1)S(1)} %collective-permute-done.9.refs_1_, bf16[256,512]{1,0:T(8,128)(2,1)S(1)} %collective-permute-done.10.refs_2_, ...), custom_call_target="tpu_custom_call" | custom-call | flops 536870912 | bytes 10334212 | tf_op jit(solution)/shard_map/mid/pallas_call | solution.py:24
  134.6 3.4 %copy-done.7 = bf16[4,512,2048]{2,1,0:T(8,128)(2,1)S(1)} copy-done((bf16[4,512,2048]{2,1,0:T(8,128)(2,1)S(1)}, bf16[4,512,2048]{2,1,0:T(8,128)(2,1)}, u32[]{:S(2)}) %copy-start.7) | copy-done | bytes 8388632
  140.4 12.5 %collective-permute-done.13.refs_2_ = bf16[256,512]{1,0:T(8,128)(2,1)S(1)} collective-permute-done((bf16[256,512]{1,0:T(8,128)(2,1)S(1)}, bf16[256,512]{1,0:T(8,128)(2,1)S(1)}, u32[]{:S(2)}, u32[]{:S(2)}) %collective-permute-start.13) | collective-permute-done | bytes 262176 | tf_op jit(solution)/shard_map/ppermute | solution.py:213
  153.0 10.9 %all_to_all.51 = f32[32,1,640]{2,1,0:T(1,128)S(1)} all-to-all(f32[32,1,640]{2,1,0:T(1,128)S(1)} %broadcast_in_dim.42), channel_id=1, replica_groups=mesh['agent'=8,'res'=4] {'res','agent'}, dimensions={0} | all-to-all | bytes 163840 | tf_op jit(solution)/shard_map/all_to_all | solution.py:224
  163.9 3.4 %copy-done.8 = bf16[4,512,2048]{2,1,0:T(8,128)(2,1)S(1)} copy-done((bf16[4,512,2048]{2,1,0:T(8,128)(2,1)S(1)}, bf16[4,512,2048]{2,1,0:T(8,128)(2,1)}, u32[]{:S(2)}) %copy-start.8) | copy-done | bytes 8388632
  167.3 2.7 %mid.7 = (f32[256,512]{1,0:T(8,128)S(1)}, f32[4,512]{1,0:T(4,128)S(1)}, f32[8,128]{1,0:T(8,128)S(1)}) custom-call(s32[1]{0:T(128)} %bitcast.1.me_ref, bf16[256,512]{1,0:T(8,128)(2,1)S(1)} %get-tuple-element.60.refs_0_, bf16[256,512]{1,0:T(8,128)(2,1)S(1)} %collective-permute-done.12.refs_1_, bf16[256,512]{1,0:T(8,128)(2,1)S(1)} %collective-permute-done.13.refs_2_, ...), custom_call_target="tpu_custom_call" | custom-call | flops 536870912 | bytes 10334212 | tf_op jit(solution)/shard_map/mid/pallas_call | solution.py:24
  170.0 3.4 %copy-done.9 = bf16[4,512,2048]{2,1,0:T(8,128)(2,1)S(1)} copy-done((bf16[4,512,2048]{2,1,0:T(8,128)(2,1)S(1)}, bf16[4,512,2048]{2,1,0:T(8,128)(2,1)}, u32[]{:S(2)}) %copy-start.9) | copy-done | bytes 8388632
  173.4 1.5 late.9
  175.6 2.6 %all-to-all-start.5 = ((f32[32,1,640]{2,1,0:T(1,128)}), f32[32,1,640]{2,1,0:T(1,128)S(1)}, u32[]{:S(2)}, u32[]{:S(2)}) async-start(f32[32,1,640]{2,1,0:T(1,128)} %broadcast_in_dim.43), calls=%async_computation.5 | async-start | bytes 163840 | tf_op jit(solution)/shard_map/all_to_all | solution.py:224
  179.4 6.4 %all-to-all-done.5 = f32[32,1,640]{2,1,0:T(1,128)S(1)} async-done(((f32[32,1,640]{2,1,0:T(1,128)}), f32[32,1,640]{2,1,0:T(1,128)S(1)}, u32[]{:S(2)}, u32[]{:S(2)}) %all-to-all-start.5) | async-done | bytes 81952 | tf_op jit(solution)/shard_map/all_to_all | solution.py:224
  (72 shorter events, 19.0 us)
Async XLA Ops:
  1.5 1.0 copy-start.10
  2.5 0.7 copy-start.11
  3.9 16.1 %collective-permute-start.1 = (bf16[256,512]{1,0:T(8,128)(2,1)S(1)}, bf16[256,512]{1,0:T(8,128)(2,1)S(1)}, u32[]{:S(2)}, u32[]{:S(2)}) collective-permute-start(bf16[256,512]{1,0:T(8,128)(2,1)S(1)} %get-tuple-element.40.refs_0_), channel_id=1, source_target_pairs={{0,2},{1,3},{2,0},{3,1},{4,6},{5,7},{6,4},{7,5},{8,10},{9,11},{10,... | collective-permute-start | bytes 786440 | tf_op jit(solution)/shard_map/ppermute | solution.py:213
  8.0 12.6 %collective-permute-start = (bf16[256,512]{1,0:T(8,128)(2,1)S(1)}, bf16[256,512]{1,0:T(8,128)(2,1)S(1)}, u32[]{:S(2)}, u32[]{:S(2)}) collective-permute-start(bf16[256,512]{1,0:T(8,128)(2,1)S(1)} %get-tuple-element.40.refs_0_), channel_id=1, source_target_pairs={{0,1},{1,0},{2,3},{3,2},{4,5},{5,4},{6,7},{7,6},{8,9},{9,8},{10,11... | collective-permute-start | bytes 786440 | tf_op jit(solution)/shard_map/ppermute | solution.py:213
  20.0 7.4 %collective-permute-start.2 = (bf16[256,512]{1,0:T(8,128)(2,1)S(1)}, bf16[256,512]{1,0:T(8,128)(2,1)S(1)}, u32[]{:S(2)}, u32[]{:S(2)}) collective-permute-start(bf16[256,512]{1,0:T(8,128)(2,1)S(1)} %collective-permute-done.1.refs_2_), channel_id=1, source_target_pairs={{0,1},{1,0},{2,3},{3,2},{4,5},{5,4},{6,7},{7,6},{8,9},{9,8},{10,11... | collective-permute-start | bytes 786440 | tf_op jit(solution)/shard_map/ppermute | solution.py:213
  20.6 3.4 %copy-start = (bf16[4,512,2048]{2,1,0:T(8,128)(2,1)S(1)}, bf16[4,512,2048]{2,1,0:T(8,128)(2,1)}, u32[]{:S(2)}) copy-start(bf16[4,512,2048]{2,1,0:T(8,128)(2,1)} %m_ref.9) | copy-start | bytes 25165828
  24.0 3.4 %copy-start.1 = (bf16[4,512,2048]{2,1,0:T(8,128)(2,1)S(1)}, bf16[4,512,2048]{2,1,0:T(8,128)(2,1)}, u32[]{:S(2)}) copy-start(bf16[4,512,2048]{2,1,0:T(8,128)(2,1)} %m_ref.9) | copy-start | bytes 25165828
  24.0 7.6 %copy-start.12 = (f32[512]{0:T(512)S(1)}, f32[512]{0:T(512)}, u32[]{:S(2)}) copy-start(f32[512]{0:T(512)} %param.11) | copy-start | bytes 6148
  24.0 7.6 %copy-start.13 = (f32[512]{0:T(512)S(1)}, f32[512]{0:T(512)}, u32[]{:S(2)}) copy-start(f32[512]{0:T(512)} %param.10) | copy-start | bytes 6148
  28.2 24.0 %collective-permute-start.4 = (bf16[256,512]{1,0:T(8,128)(2,1)S(1)}, bf16[256,512]{1,0:T(8,128)(2,1)S(1)}, u32[]{:S(2)}, u32[]{:S(2)}) collective-permute-start(bf16[256,512]{1,0:T(8,128)(2,1)S(1)} %get-tuple-element.43.refs_0_), channel_id=1, source_target_pairs={{0,2},{1,3},{2,0},{3,1},{4,6},{5,7},{6,4},{7,5},{8,10},{9,11},{10,... | collective-permute-start | bytes 786440 | tf_op jit(solution)/shard_map/ppermute | solution.py:213
  32.4 15.6 %all-to-all-start.1 = ((f32[32,1,1024]{2,1,0:T(1,128)}), f32[32,1,1024]{2,1,0:T(1,128)S(1)}, u32[]{:S(2)}, u32[]{:S(2)}) async-start(f32[32,1,1024]{2,1,0:T(1,128)} %broadcast_in_dim.17), calls=%async_computation.1 | async-start | bytes 262144 | tf_op jit(solution)/shard_map/all_to_all | solution.py:224
  36.1 24.0 %collective-permute-start.3 = (bf16[256,512]{1,0:T(8,128)(2,1)S(1)}, bf16[256,512]{1,0:T(8,128)(2,1)S(1)}, u32[]{:S(2)}, u32[]{:S(2)}) collective-permute-start(bf16[256,512]{1,0:T(8,128)(2,1)S(1)} %get-tuple-element.43.refs_0_), channel_id=1, source_target_pairs={{0,1},{1,0},{2,3},{3,2},{4,5},{5,4},{6,7},{7,6},{8,9},{9,8},{10,11... | collective-permute-start | bytes 786440 | tf_op jit(solution)/shard_map/ppermute | solution.py:213
  48.8 11.4 %all-to-all-start = ((f32[32,1,640]{2,1,0:T(1,128)}), f32[32,1,640]{2,1,0:T(1,128)S(1)}, u32[]{:S(2)}, u32[]{:S(2)}) async-start(f32[32,1,640]{2,1,0:T(1,128)} %broadcast_in_dim.16), calls=%async_computation | async-start | bytes 163840 | tf_op jit(solution)/shard_map/all_to_all | solution.py:224
  52.3 14.0 %collective-permute-start.5 = (bf16[256,512]{1,0:T(8,128)(2,1)S(1)}, bf16[256,512]{1,0:T(8,128)(2,1)S(1)}, u32[]{:S(2)}, u32[]{:S(2)}) collective-permute-start(bf16[256,512]{1,0:T(8,128)(2,1)S(1)} %collective-permute-done.4.refs_2_), channel_id=1, source_target_pairs={{0,1},{1,0},{2,3},{3,2},{4,5},{5,4},{6,7},{7,6},{8,9},{9,8},{10,11... | collective-permute-start | bytes 786440 | tf_op jit(solution)/shard_map/ppermute | solution.py:213
  60.2 3.4 %copy-start.2 = (bf16[4,512,2048]{2,1,0:T(8,128)(2,1)S(1)}, bf16[4,512,2048]{2,1,0:T(8,128)(2,1)}, u32[]{:S(2)}) copy-start(bf16[4,512,2048]{2,1,0:T(8,128)(2,1)} %m_ref.9) | copy-start | bytes 25165828
  63.6 3.4 %copy-start.3 = (bf16[4,512,2048]{2,1,0:T(8,128)(2,1)S(1)}, bf16[4,512,2048]{2,1,0:T(8,128)(2,1)}, u32[]{:S(2)}) copy-start(bf16[4,512,2048]{2,1,0:T(8,128)(2,1)} %m_ref.9) | copy-start | bytes 25165828
  67.8 14.1 %collective-permute-start.7 = (bf16[256,512]{1,0:T(8,128)(2,1)S(1)}, bf16[256,512]{1,0:T(8,128)(2,1)S(1)}, u32[]{:S(2)}, u32[]{:S(2)}) collective-permute-start(bf16[256,512]{1,0:T(8,128)(2,1)S(1)} %get-tuple-element.48.refs_0_), channel_id=1, source_target_pairs={{0,2},{1,3},{2,0},{3,1},{4,6},{5,7},{6,4},{7,5},{8,10},{9,11},{10,... | collective-permute-start | bytes 786440 | tf_op jit(solution)/shard_map/ppermute | solution.py:213
  68.7 24.0 %collective-permute-start.6 = (bf16[256,512]{1,0:T(8,128)(2,1)S(1)}, bf16[256,512]{1,0:T(8,128)(2,1)S(1)}, u32[]{:S(2)}, u32[]{:S(2)}) collective-permute-start(bf16[256,512]{1,0:T(8,128)(2,1)S(1)} %get-tuple-element.48.refs_0_), channel_id=1, source_target_pairs={{0,1},{1,0},{2,3},{3,2},{4,5},{5,4},{6,7},{7,6},{8,9},{9,8},{10,11... | collective-permute-start | bytes 786440 | tf_op jit(solution)/shard_map/ppermute | solution.py:213
  81.9 16.8 %collective-permute-start.8 = (bf16[256,512]{1,0:T(8,128)(2,1)S(1)}, bf16[256,512]{1,0:T(8,128)(2,1)S(1)}, u32[]{:S(2)}, u32[]{:S(2)}) collective-permute-start(bf16[256,512]{1,0:T(8,128)(2,1)S(1)} %collective-permute-done.7.refs_2_), channel_id=1, source_target_pairs={{0,1},{1,0},{2,3},{3,2},{4,5},{5,4},{6,7},{7,6},{8,9},{9,8},{10,11... | collective-permute-start | bytes 786440 | tf_op jit(solution)/shard_map/ppermute | solution.py:213
  92.6 3.4 %copy-start.4 = (bf16[4,512,2048]{2,1,0:T(8,128)(2,1)S(1)}, bf16[4,512,2048]{2,1,0:T(8,128)(2,1)}, u32[]{:S(2)}) copy-start(bf16[4,512,2048]{2,1,0:T(8,128)(2,1)} %m_ref.9) | copy-start | bytes 25165828
  98.7 3.4 %copy-start.5 = (bf16[4,512,2048]{2,1,0:T(8,128)(2,1)S(1)}, bf16[4,512,2048]{2,1,0:T(8,128)(2,1)}, u32[]{:S(2)}) copy-start(bf16[4,512,2048]{2,1,0:T(8,128)(2,1)} %m_ref.9) | copy-start | bytes 25165828
  102.9 14.2 %collective-permute-start.10 = (bf16[256,512]{1,0:T(8,128)(2,1)S(1)}, bf16[256,512]{1,0:T(8,128)(2,1)S(1)}, u32[]{:S(2)}, u32[]{:S(2)}) collective-permute-start(bf16[256,512]{1,0:T(8,128)(2,1)S(1)} %get-tuple-element.54.refs_0_), channel_id=1, source_target_pairs={{0,2},{1,3},{2,0},{3,1},{4,6},{5,7},{6,4},{7,5},{8,10},{9,11},{10,... | collective-permute-start | bytes 786440 | tf_op jit(solution)/shard_map/ppermute | solution.py:213
  103.7 24.8 %collective-permute-start.9 = (bf16[256,512]{1,0:T(8,128)(2,1)S(1)}, bf16[256,512]{1,0:T(8,128)(2,1)S(1)}, u32[]{:S(2)}, u32[]{:S(2)}) collective-permute-start(bf16[256,512]{1,0:T(8,128)(2,1)S(1)} %get-tuple-element.54.refs_0_), channel_id=1, source_target_pairs={{0,1},{1,0},{2,3},{3,2},{4,5},{5,4},{6,7},{7,6},{8,9},{9,8},{10,11... | collective-permute-start | bytes 786440 | tf_op jit(solution)/shard_map/ppermute | solution.py:213
  117.1 17.4 %collective-permute-start.11 = (bf16[256,512]{1,0:T(8,128)(2,1)S(1)}, bf16[256,512]{1,0:T(8,128)(2,1)S(1)}, u32[]{:S(2)}, u32[]{:S(2)}) collective-permute-start(bf16[256,512]{1,0:T(8,128)(2,1)S(1)} %collective-permute-done.10.refs_2_), channel_id=1, source_target_pairs={{0,1},{1,0},{2,3},{3,2},{4,5},{5,4},{6,7},{7,6},{8,9},{9,8},{10,11... | collective-permute-start | bytes 786440 | tf_op jit(solution)/shard_map/ppermute | solution.py:213
  128.5 3.4 %copy-start.6 = (bf16[4,512,2048]{2,1,0:T(8,128)(2,1)S(1)}, bf16[4,512,2048]{2,1,0:T(8,128)(2,1)}, u32[]{:S(2)}) copy-start(bf16[4,512,2048]{2,1,0:T(8,128)(2,1)} %m_ref.9) | copy-start | bytes 25165828
  134.5 3.4 %copy-start.7 = (bf16[4,512,2048]{2,1,0:T(8,128)(2,1)S(1)}, bf16[4,512,2048]{2,1,0:T(8,128)(2,1)}, u32[]{:S(2)}) copy-start(bf16[4,512,2048]{2,1,0:T(8,128)(2,1)} %m_ref.9) | copy-start | bytes 25165828
  138.7 14.2 %collective-permute-start.13 = (bf16[256,512]{1,0:T(8,128)(2,1)S(1)}, bf16[256,512]{1,0:T(8,128)(2,1)S(1)}, u32[]{:S(2)}, u32[]{:S(2)}) collective-permute-start(bf16[256,512]{1,0:T(8,128)(2,1)S(1)} %get-tuple-element.60.refs_0_), channel_id=1, source_target_pairs={{0,2},{1,3},{2,0},{3,1},{4,6},{5,7},{6,4},{7,5},{8,10},{9,11},{10,... | collective-permute-start | bytes 786440 | tf_op jit(solution)/shard_map/ppermute | solution.py:213
  139.5 24.4 %collective-permute-start.12 = (bf16[256,512]{1,0:T(8,128)(2,1)S(1)}, bf16[256,512]{1,0:T(8,128)(2,1)S(1)}, u32[]{:S(2)}, u32[]{:S(2)}) collective-permute-start(bf16[256,512]{1,0:T(8,128)(2,1)S(1)} %get-tuple-element.60.refs_0_), channel_id=1, source_target_pairs={{0,1},{1,0},{2,3},{3,2},{4,5},{5,4},{6,7},{7,6},{8,9},{9,8},{10,11... | collective-permute-start | bytes 786440 | tf_op jit(solution)/shard_map/ppermute | solution.py:213
  152.9 17.1 %collective-permute-start.14 = (bf16[256,512]{1,0:T(8,128)(2,1)S(1)}, bf16[256,512]{1,0:T(8,128)(2,1)S(1)}, u32[]{:S(2)}, u32[]{:S(2)}) collective-permute-start(bf16[256,512]{1,0:T(8,128)(2,1)S(1)} %collective-permute-done.13.refs_2_), channel_id=1, source_target_pairs={{0,1},{1,0},{2,3},{3,2},{4,5},{5,4},{6,7},{7,6},{8,9},{9,8},{10,11... | collective-permute-start | bytes 786440 | tf_op jit(solution)/shard_map/ppermute | solution.py:213
  163.9 3.4 %copy-start.8 = (bf16[4,512,2048]{2,1,0:T(8,128)(2,1)S(1)}, bf16[4,512,2048]{2,1,0:T(8,128)(2,1)}, u32[]{:S(2)}) copy-start(bf16[4,512,2048]{2,1,0:T(8,128)(2,1)} %m_ref.9) | copy-start | bytes 25165828
  170.0 3.4 %copy-start.9 = (bf16[4,512,2048]{2,1,0:T(8,128)(2,1)S(1)}, bf16[4,512,2048]{2,1,0:T(8,128)(2,1)}, u32[]{:S(2)}) copy-start(bf16[4,512,2048]{2,1,0:T(8,128)(2,1)} %m_ref.9) | copy-start | bytes 25165828
  175.6 10.2 %all-to-all-start.5 = ((f32[32,1,640]{2,1,0:T(1,128)}), f32[32,1,640]{2,1,0:T(1,128)S(1)}, u32[]{:S(2)}, u32[]{:S(2)}) async-start(f32[32,1,640]{2,1,0:T(1,128)} %broadcast_in_dim.43), calls=%async_computation.5 | async-start | bytes 163840 | tf_op jit(solution)/shard_map/all_to_all | solution.py:224

commit v2 on v1

v2 whole, which is shorter than its diff:
```python
import functools

import jax
import jax.numpy as jnp
from jax import lax
from jax.experimental import pallas as pl
from jax.experimental.pallas import tpu as pltpu
from jax.sharding import PartitionSpec as P

ITERS = 5
LANES = 128

penalty = 1.0
eps = 1e-06

VMEM = pl.BlockSpec(memory_space=pltpu.VMEM)
SMEM = pl.BlockSpec(memory_space=pltpu.SMEM)
HBM = pl.BlockSpec(memory_space=pltpu.HBM)
F32 = jnp.float32
BF16 = jnp.bfloat16


def call(body, out_shape, args, scalars=0, far=(), name=None, flops=0, limit=24 << 20, scratch=()):
    moved = sum(a.size * a.dtype.itemsize for a in args)
    args = [pltpu.with_memory_space_constraint(a, pltpu.HBM) if at in far else a for at, a in enumerate(args)]
    spaces = [HBM if at in far else SMEM if at < scalars else VMEM for at in range(len(args))]
    return pl.pallas_call(
        body,
        out_shape=out_shape,
        in_specs=spaces,
        out_specs=jax.tree.map(lambda _: VMEM, out_shape),
        scratch_shapes=scratch,
        compiler_params=pltpu.CompilerParams(vmem_limit_bytes=limit),
        cost_estimate=pl.CostEstimate(flops=flops, bytes_accessed=moved, transcendentals=0),
        name=name,
    )(*args)


def shaped(shape, dtype):
    return jax.ShapeDtypeStruct(shape, dtype)


def split(value):
    high = value.astype(BF16)
    return high, (value - high.astype(F32)).astype(BF16)


def three(value):
    high = value.astype(BF16)
    rest = value - high.astype(F32)
    middle = rest.astype(BF16)
    return high, middle, (rest - middle.astype(F32)).astype(BF16)


def prep_kernel(types, cost_far, kind_far, mask_far, high_ref, low_ref, expand_ref, sort_ref, cost_ref, kind_ref, mask_ref, sems):
    copies = [
        pltpu.make_async_copy(far, near, sems.at[at])
        for at, (far, near) in enumerate(((kind_far, kind_ref), (mask_far, mask_ref), (cost_far, cost_ref)))
    ]
    for copy in copies:
        copy.start()
    agents, width = cost_ref.shape
    blocks = mask_ref.shape[0]
    copies[0].wait()
    kind = kind_ref[...]
    row = lax.broadcasted_iota(jnp.int32, (agents, agents), 0)
    column = lax.broadcasted_iota(jnp.int32, (agents, agents), 1)
    earlier = (row < column).astype(F32).astype(BF16)
    type_of = lax.broadcasted_iota(jnp.int32, (16, agents), 0)
    member = (jnp.broadcast_to(kind, (16, agents)) == type_of).astype(F32)
    rank = jnp.dot(member.astype(BF16), earlier, preferred_element_type=F32)
    start = type_of.astype(F32) * (agents // types)
    place = jnp.sum(member * (rank + start), axis=0, keepdims=True)
    sort = (row.astype(F32) == jnp.broadcast_to(place, (agents, agents))).astype(F32).astype(BF16)
    sort_ref[...] = sort
    copies[2].wait()
    high, low = split(-cost_ref[...])
    high_ref[...] = jnp.dot(sort, high, preferred_element_type=F32).astype(BF16)
    low_ref[...] = jnp.dot(sort, low, preferred_element_type=F32).astype(BF16)
    copies[1].wait()
    mask = lax.dot_general(
        sort, mask_ref[...].astype(F32).astype(BF16), (((1,), (1,)), ((), ())), preferred_element_type=F32
    )
    each = width // blocks
    for block in range(blocks):
        expand_ref[:, block * each:(block + 1) * each] = jnp.broadcast_to(
            mask[:, block:block + 1], (agents, each)
        )


def times(left, right):
    return lax.dot_general(left, right, (((1,), (1,)), ((), ())), preferred_element_type=F32)


def fetch(m_far, m_ref, last_ref, sems, me):
    slots, types, width = m_ref.shape[0] + 1, m_ref.shape[1], m_ref.shape[2]
    copies = {}
    for kind in range(types):
        for slot in range(slots):
            at = pl.multiple_of((me ^ slot) * width, LANES)
            copies[slot, kind] = pltpu.make_async_copy(
                m_far.at[kind, :, pl.ds(at, width)],
                last_ref.at[kind] if slot == slots - 1 else m_ref.at[slot, kind],
                sems.at[slot, kind],
            )
            copies[slot, kind].start()
    return copies


def first_kernel(slots, me_ref, *refs):
    low_ref, m_far, acc_ref, last_ref, m_ref, sems = refs[slots:]
    types = m_ref.shape[1]
    group = low_ref.shape[0] // types
    copies = fetch(m_far, m_ref, last_ref, sems, me_ref[0])
    for kind in range(types):
        rows = slice(kind * group, (kind + 1) * group)
        copies[0, kind].wait()
        own = times(jnp.concatenate([refs[0][rows], low_ref[rows]], axis=0), m_ref[0, kind])
        total = own[:group] + own[group:]
        for slot in range(1, slots):
            copies[slot, kind].wait()
            total += times(refs[slot][rows], m_ref[slot, kind])
        copies[slots, kind].wait()
        acc_ref[rows] = total


def vectors(received_ref, weight, target, prices, per_block, count):
    width = weight.shape[1]
    parts, changes = [], []
    blocks = weight.shape[0]
    for block in range(blocks):
        rows = jnp.sum(received_ref[block * per_block:(block + 1) * per_block], axis=0)
        parts.append(rows[:, :width])
        changes.append(rows[:, width:])
    mean = jnp.concatenate(parts, axis=0) / count
    shared = (weight * target + penalty * (prices + mean)) / (weight + penalty)
    prices = prices + mean - shared
    gap = mean - shared
    primal = count * jnp.sum(gap * gap)
    dual = penalty * penalty * jnp.sum(sum(changes))
    return mean, shared, prices, primal, dual


def norms_of(norms, step, primal, dual):
    lane = lax.broadcasted_iota(jnp.int32, norms.shape, 1)
    row = lax.broadcasted_iota(jnp.int32, norms.shape, 0)
    norms = jnp.where((lane == step) & (row == 0), jnp.sqrt(primal + eps), norms)
    return jnp.where((lane == step) & (row == 1), jnp.sqrt(dual + eps), norms)


def mid_kernel(slots, step, per_block, count, me_ref, *refs):
    usage_ref, received_ref, weight_ref, target_ref, prices_ref, norms_ref, base_ref, m_far = refs[slots:slots + 8]
    acc_ref, new_prices_ref, new_norms_ref, last_ref, v_ref, m_ref, sems = refs[slots + 8:]
    types, width = m_ref.shape[1:3]
    group = base_ref.shape[0] // types
    me = me_ref[0]
    copies = fetch(m_far, m_ref, last_ref, sems, me)
    mean, shared, prices, primal, dual = vectors(
        received_ref, weight_ref[...], target_ref[...], prices_ref[...], per_block, count
    )
    new_prices_ref[...] = prices
    new_norms_ref[...] = norms_of(norms_ref[...], step, primal, dual)
    v_ref[...] = shared - mean - prices
    row = lax.broadcasted_iota(jnp.int32, (16, width), 0)
    lefts = []
    for slot in range(slots + 1):
        value = v_ref[pl.ds(me ^ slot, 1), :]
        high, middle, low = (jnp.broadcast_to(x.astype(F32), (16, width)) for x in three(value))
        lefts.append(
            jnp.where(row == 0, high, jnp.where(row == 1, middle, jnp.where(row == 2, low, 0.0))).astype(BF16)
        )
    for kind in range(types):
        rows = slice(kind * group, (kind + 1) * group)
        own_high = refs[0][rows]
        own_low = (usage_ref[rows] - own_high.astype(F32)).astype(BF16)
        copies[0, kind].wait()
        own = times(jnp.concatenate([own_high, own_low, lefts[0]], axis=0), m_ref[0, kind])
        total = own[:group] + own[group:2 * group]
        shift = own[2 * group:]
        for slot in range(1, slots):
            copies[slot, kind].wait()
            got = times(jnp.concatenate([refs[slot][rows], lefts[slot]], axis=0), m_ref[slot, kind])
            total += got[:group]
            shift += got[group:]
        copies[slots, kind].wait()
        shift += times(lefts[slots], last_ref[kind])
        acc_ref[rows] = base_ref[rows] + total + jnp.sum(shift, axis=0, keepdims=True)


def late_kernel(first, final, acc_ref, slot_ref, expand_ref, usage_ref, last_ref, new_ref, payload_ref, *rest):
    types, width = last_ref.shape[:2]
    group = acc_ref.shape[0] // types
    sums = jnp.zeros((8, width), F32)
    change = jnp.zeros((8, width), F32)
    for kind in range(types):
        rows = slice(kind * group, (kind + 1) * group)
        total = acc_ref[rows] + times(slot_ref[rows], last_ref[kind])
        new = expand_ref[rows] * total
        new_ref[rows] = new
        if not final:
            rest[0][rows] = new.astype(BF16)
        if first:
            rest[1][rows] = total
        moved = new if first else new - usage_ref[rows]
        sums += jnp.sum(new.reshape(group // 8, 8, width), axis=0)
        change += jnp.sum((moved * moved).reshape(group // 8, 8, width), axis=0)
    lanes = sum(change[:, at:at + LANES] for at in range(0, width, LANES))
    row = jnp.concatenate(
        [jnp.sum(sums, axis=0, keepdims=True), jnp.sum(lanes, axis=0, keepdims=True)], axis=1
    )
    payload_ref[...] = jnp.broadcast_to(row[None], payload_ref.shape)


def last_kernel(step, per_block, count, me_ref, received_ref, weight_ref, target_ref, prices_ref, norms_ref,
                own_shared_ref, own_prices_ref, new_norms_ref, keep_ref):
    mean, shared, prices, primal, dual = vectors(
        received_ref, weight_ref[...], target_ref[...], prices_ref[...], per_block, count
    )
    new_norms_ref[...] = norms_of(norms_ref[...], step, primal, dual)
    keep_ref[...] = shared
    own_shared_ref[...] = keep_ref[pl.ds(me_ref[0], 1), :]
    keep_ref[...] = prices
    own_prices_ref[...] = keep_ref[pl.ds(me_ref[0], 1), :]


def restore_kernel(sort_ref, usage_ref, out_ref):
    total = None
    for piece in three(usage_ref[...]):
        got = lax.dot_general(sort_ref[...], piece, (((0,), (0,)), ((), ())), preferred_element_type=F32)
        total = got if total is None else total + got
    out_ref[...] = total


def on_device(linear_cost, agent_type, block_mask, inverses, cost_weight, target):
    agents, width = linear_cost.shape
    types = inverses.shape[0]
    per_block = lax.axis_size("agent")
    blocks = lax.axis_size("res")
    count = agents * per_block
    me = lax.axis_index("res").astype(jnp.int32).reshape(1)
    flops = 2 * agents * width * width

    def swap(value, bit):
        return lax.ppermute(value, "res", [(i, i ^ bit) for i in range(blocks)])

    def gather(own, row):
        slots = [own] + [None] * (blocks - 1)
        order = sorted(range(1, blocks), key=lambda m: (bin(m).count("1"), -m))
        received = None
        for slot in order:
            bit = slot & -slot
            source = slots[slot ^ bit]
            if slot ^ bit and received is None:
                received = spread(row)
                source, received = lax.optimization_barrier((source, received))
            slots[slot] = swap(source, bit)
        return slots, received

    def spread(rows):
        return lax.all_to_all(rows, ("res", "agent"), 0, 0)

    high, low, expand, sort = call(
        functools.partial(prep_kernel, types),
        (shaped((agents, width), BF16), shaped((agents, width), BF16), shaped((agents, width), F32), shaped((agents, agents), BF16)),
        (linear_cost, agent_type.reshape(1, agents), block_mask.T),
        far=(0, 1, 2), name="prep",
        scratch=[
            pltpu.VMEM((agents, width), F32),
            pltpu.VMEM((1, agents), jnp.int32),
            pltpu.VMEM(block_mask.shape[::-1], jnp.int32),
            pltpu.SemaphoreType.DMA((3,)),
        ],
    )
    pair = jnp.concatenate([cost_weight, target]).reshape(1, 1, 2 * width)
    slots, both = gather(high, jnp.broadcast_to(pair, (blocks * per_block, 1, 2 * width)))
    both = both[::per_block, 0]
    weights, targets = both[:, :width], both[:, width:]
    prices = jnp.zeros((blocks, width), F32)
    norms = jnp.zeros((8, LANES), F32)
    matrices = [
        pltpu.VMEM((blocks - 1, types, width, width), BF16),
        pltpu.SemaphoreType.DMA((blocks, types)),
    ]
    last_matrices = shaped((types, width, width), BF16)
    whole = shaped((agents, width), F32)
    base = usage = None
    for step in range(ITERS):
        if step == 0:
            acc, last = call(
                functools.partial(first_kernel, blocks - 1),
                (whole, last_matrices),
                (me, *slots[:-1], low, inverses),
                scalars=1, far=(blocks + 1,), name="first", flops=flops * blocks, scratch=matrices,
            )
        else:
            acc, prices, norms, last = call(
                functools.partial(mid_kernel, blocks - 1, step - 1, per_block, count),
                (whole, shaped((blocks, width), F32), shaped((8, LANES), F32), last_matrices),
                (me, *slots[:-1], usage, received, weights, targets, prices, norms, base, inverses),
                scalars=1, far=(blocks + 7,), name="mid", flops=flops * blocks,
                scratch=[pltpu.VMEM((blocks, width), F32)] + matrices,
            )
        outs = (whole, shaped((blocks * per_block, 1, width + LANES), F32))
        if step < ITERS - 1:
            outs += (shaped((agents, width), BF16),)
        if step == 0:
            outs += (whole,)
        got = call(
            functools.partial(late_kernel, step == 0, step == ITERS - 1),
            outs,
            (acc, slots[-1], expand, acc if usage is None else usage, last),
            name="late", flops=flops,
        )
        usage, payload = got[:2]
        if step == 0:
            base = got[3]
        if step < ITERS - 1:
            slots, received = gather(got[2], payload)
        else:
            received = spread(payload)
    own_shared, own_prices, norms = call(
        functools.partial(last_kernel, ITERS - 1, per_block, count),
        (shaped((1, width), F32), shaped((1, width), F32), shaped((8, LANES), F32)),
        (me, received, weights, targets, prices, norms),
        scalars=1, name="last",
        scratch=[pltpu.VMEM((blocks, width), F32)],
    )
    out = call(restore_kernel, shaped((agents, width), F32), (sort, usage), name="restore")
    return out, own_shared.reshape(width), own_prices.reshape(width), norms[0, :ITERS], norms[1, :ITERS]


def solution(mesh):
    placed = (
        P("agent", "res"),
        P("agent"),
        P("agent", "res"),
        P(None, "res", None),
        P("res"),
        P("res"),
    )
    return jax.shard_map(
        on_device,
        mesh=mesh,
        in_specs=placed,
        out_specs=(P("agent", "res"), P("res"), P("res"), P(), P()),
        check_vma=False,
    )
```

time: 188 us -> 159 us (0.85)
  blocking collectives: 32.8 us -> 0 us
  local copies, waits for them, and re-layouts: 33.1 us -> 1.3 us
  starting transfers between devices: 28.4 us -> 53.7 us
  Pallas kernels: 20 us -> 34.7 us
  waiting for transfers between devices: 71.6 us -> 67.2 us
    ppermute x15, waiting for transfers between devices: 49.2 us -> 13.2 us  [swap(): return lax.ppermute(value, 'res', [(i, i ^ bit) for i in range(blocks)])]
    all_to_all x3 -> x0, blocking collectives: 32.8 us -> none  [spread(): return lax.all_to_all(rows, ('res', 'agent'), 0, 0, tiled=True)]
    all_to_all x3 -> x6, waiting for transfers between devices: 22.4 us -> 54 us  [spread(): return lax.all_to_all(rows, ('res', 'agent'), 0, 0)]
    unnamed x35 -> x0, local copies, waits for them, and re-layouts: 30.3 us -> none
    all_to_all x3 -> x6, starting transfers between devices: 9.79 us -> 28.6 us  [spread(): return lax.all_to_all(rows, ('res', 'agent'), 0, 0)]
    pallas_call x13, Pallas kernels: 20 us -> 34.7 us  [call(): pl.pallas_call(body, out_shape=out_shape, in_specs=spaces, out_specs=jax....]
    ppermute x15, starting transfers between devices: 18.6 us -> 25.2 us  [swap(): return lax.ppermute(value, 'res', [(i, i ^ bit) for i in range(blocks)])]
  transfers between devices with their start and end apart: 18 -> 21, of which waited for: 8 -> 16; matrix products, arithmetic and copies ran while one was open for 1% -> 1% of each run, Pallas kernels for 7% -> 16%
where the time goes in v2:
time: 159 us; the launch traced here: 158 us
  waiting for transfers between devices  67.2 us (42%)
  starting transfers between devices  53.7 us (34%)
  Pallas kernels  34.7 us (22%)
    all_to_all x6, waiting for transfers between devices, spread(): return lax.all_to_all(rows, ('res', 'agent'), 0, 0)  54 us
    pallas_call x13, Pallas kernels, call(): pl.pallas_call(body, out_shape=out_shape, in_specs=spaces, out_specs=jax....  34.7 us
    all_to_all x6, starting transfers between devices, spread(): return lax.all_to_all(rows, ('res', 'agent'), 0, 0)  28.6 us
    ppermute x15, starting transfers between devices, swap(): return lax.ppermute(value, 'res', [(i, i ^ bit) for i in range(blocks)])  25.2 us
    ppermute x15, waiting for transfers between devices, swap(): return lax.ppermute(value, 'res', [(i, i ^ bit) for i in range(blocks)])  13.2 us
  transfers between devices with their start and end apart: 21, of which 16 were waited for; matrix products, arithmetic and copies ran while one was open for 1% of the time, Pallas kernels for 16%

profile of v2, /device:TPU:0, one launch (start us, length us, event | category | flops | bytes accessed | tf_op | source)
XLA Modules:
  0.0 158.4 jit_solution(14400468384815825514)
XLA Ops:
  0.6 1.8 %prep.1 = (bf16[256,512]{1,0:T(8,128)(2,1)S(1)}, bf16[256,512]{1,0:T(8,128)(2,1)S(1)}, f32[256,512]{1,0:T(8,128)S(1)}, bf16[256,256]{1,0:T(8,128)(2,1)S(1)}) custom-call(f32[256,512]{1,0:T(8,128)} %cost_far.1, s32[1,256]{1,0:T(1,128)} %bitcast.12, s32[4,256]{1,0:T(4,128)} %bitcast.11), custom_call_target="tpu_custom_call" | custom-call | bytes 529408 | tf_op jit(solution)/shard_map/prep/pallas_call | solution.py:27
  2.4 4.1 %collective-permute-start.1 = (bf16[256,512]{1,0:T(8,128)(2,1)S(1)}, bf16[256,512]{1,0:T(8,128)(2,1)S(1)}, u32[]{:S(2)}, u32[]{:S(2)}) collective-permute-start(bf16[256,512]{1,0:T(8,128)(2,1)S(1)} %get-tuple-element.56.refs_0_), channel_id=1, source_target_pairs={{0,2},{1,3},{2,0},{3,1},{4,6},{5,7},{6,4},{7,5},{8,10},{9,11},{10,... | collective-permute-start | bytes 786440 | tf_op jit(solution)/shard_map/ppermute | solution.py:244
  8.0 3.8 %all-to-all-start = ((f32[32,1,1024]{2,1,0:T(1,128)}), f32[32,1,1024]{2,1,0:T(1,128)S(1)}, u32[]{:S(2)}, u32[]{:S(2)}) async-start(f32[32,1,1024]{2,1,0:T(1,128)} %broadcast_in_dim.11), calls=%async_computation | async-start | bytes 262144 | tf_op jit(solution)/shard_map/all_to_all | solution.py:260
  11.8 1.8 %collective-permute-start = (bf16[256,512]{1,0:T(8,128)(2,1)S(1)}, bf16[256,512]{1,0:T(8,128)(2,1)S(1)}, u32[]{:S(2)}, u32[]{:S(2)}) collective-permute-start(bf16[256,512]{1,0:T(8,128)(2,1)S(1)} %get-tuple-element.56.refs_0_), channel_id=1, source_target_pairs={{0,1},{1,0},{2,3},{3,2},{4,5},{5,4},{6,7},{7,6},{8,9},{9,8},{10,11... | collective-permute-start | bytes 786440 | tf_op jit(solution)/shard_map/ppermute | solution.py:244
  13.7 9.4 %all-to-all-done = f32[32,1,1024]{2,1,0:T(1,128)S(1)} async-done(((f32[32,1,1024]{2,1,0:T(1,128)}), f32[32,1,1024]{2,1,0:T(1,128)S(1)}, u32[]{:S(2)}, u32[]{:S(2)}) %all-to-all-start) | async-done | bytes 131104 | tf_op jit(solution)/shard_map/all_to_all | solution.py:260
  23.7 2.6 %collective-permute-done.refs_1_ = bf16[256,512]{1,0:T(8,128)(2,1)S(1)} collective-permute-done((bf16[256,512]{1,0:T(8,128)(2,1)S(1)}, bf16[256,512]{1,0:T(8,128)(2,1)S(1)}, u32[]{:S(2)}, u32[]{:S(2)}) %collective-permute-start) | collective-permute-done | bytes 262176 | tf_op jit(solution)/shard_map/ppermute | solution.py:244
  26.2 3.8 %first.1 = (f32[256,512]{1,0:T(8,128)S(1)}, bf16[4,512,512]{2,1,0:T(8,128)(2,1)S(1)}) custom-call(s32[1]{0:T(128)} %bitcast.2.me_ref, bf16[256,512]{1,0:T(8,128)(2,1)S(1)} %get-tuple-element.56.refs_0_, bf16[256,512]{1,0:T(8,128)(2,1)S(1)} %collective-permute-done.refs_1_, bf16[256,512]{1,0:T(8,128)(2,1)S(1)} %collective-permute-done.1.refs_2_, ...), custom_call_target="tpu_custom_call" | custom-call | flops 536870912 | bytes 9437188 | tf_op jit(solution)/shard_map/first/pallas_call | solution.py:27
  30.1 1.7 %collective-permute-done.2.slot_ref = bf16[256,512]{1,0:T(8,128)(2,1)S(1)} collective-permute-done((bf16[256,512]{1,0:T(8,128)(2,1)S(1)}, bf16[256,512]{1,0:T(8,128)(2,1)S(1)}, u32[]{:S(2)}, u32[]{:S(2)}) %collective-permute-start.2) | collective-permute-done | bytes 262176 | tf_op jit(solution)/shard_map/ppermute | solution.py:244
  33.2 2.0 %collective-permute-start.4 = (bf16[256,512]{1,0:T(8,128)(2,1)S(1)}, bf16[256,512]{1,0:T(8,128)(2,1)S(1)}, u32[]{:S(2)}, u32[]{:S(2)}) collective-permute-start(bf16[256,512]{1,0:T(8,128)(2,1)S(1)} %get-tuple-element.62.refs_0_), channel_id=1, source_target_pairs={{0,2},{1,3},{2,0},{3,1},{4,6},{5,7},{6,4},{7,5},{8,10},{9,11},{10,... | collective-permute-start | bytes 786440 | tf_op jit(solution)/shard_map/ppermute | solution.py:244
  35.2 4.4 %all-to-all-start.1 = ((f32[32,1,640]{2,1,0:T(1,128)}), f32[32,1,640]{2,1,0:T(1,128)S(1)}, u32[]{:S(2)}, u32[]{:S(2)}) async-start(f32[32,1,640]{2,1,0:T(1,128)} %get-tuple-element.64), calls=%async_computation.1 | async-start | bytes 163840 | tf_op jit(solution)/shard_map/all_to_all | solution.py:260
  39.6 1.8 %collective-permute-start.3 = (bf16[256,512]{1,0:T(8,128)(2,1)S(1)}, bf16[256,512]{1,0:T(8,128)(2,1)S(1)}, u32[]{:S(2)}, u32[]{:S(2)}) collective-permute-start(bf16[256,512]{1,0:T(8,128)(2,1)S(1)} %get-tuple-element.62.refs_0_), channel_id=1, source_target_pairs={{0,1},{1,0},{2,3},{3,2},{4,5},{5,4},{6,7},{7,6},{8,9},{9,8},{10,11... | collective-permute-start | bytes 786440 | tf_op jit(solution)/shard_map/ppermute | solution.py:244
  41.5 10.1 %all-to-all-done.1.refs_4_ = f32[32,1,640]{2,1,0:T(1,128)S(1)} async-done(((f32[32,1,640]{2,1,0:T(1,128)}), f32[32,1,640]{2,1,0:T(1,128)S(1)}, u32[]{:S(2)}, u32[]{:S(2)}) %all-to-all-start.1) | async-done | bytes 81952 | tf_op jit(solution)/shard_map/all_to_all | solution.py:260
  53.7 5.0 %mid.4 = (f32[256,512]{1,0:T(8,128)S(1)}, f32[4,512]{1,0:T(4,128)S(1)}, f32[8,128]{1,0:T(8,128)S(1)}, bf16[4,512,512]{2,1,0:T(8,128)(2,1)S(1)}) custom-call(s32[1]{0:T(128)} %bitcast.2.me_ref, bf16[256,512]{1,0:T(8,128)(2,1)S(1)} %get-tuple-element.62.refs_0_, bf16[256,512]{1,0:T(8,128)(2,1)S(1)} %collective-permute-done.3.refs_1_, ...), custom_call_target="tpu_custom_call" | custom-call | flops 536870912 | bytes 10334212 | tf_op jit(solution)/shard_map/mid/pallas_call | solution.py:27
  60.8 1.9 %collective-permute-start.7 = (bf16[256,512]{1,0:T(8,128)(2,1)S(1)}, bf16[256,512]{1,0:T(8,128)(2,1)S(1)}, u32[]{:S(2)}, u32[]{:S(2)}) collective-permute-start(bf16[256,512]{1,0:T(8,128)(2,1)S(1)} %get-tuple-element.71.refs_0_), channel_id=1, source_target_pairs={{0,2},{1,3},{2,0},{3,1},{4,6},{5,7},{6,4},{7,5},{8,10},{9,11},{10,... | collective-permute-start | bytes 786440 | tf_op jit(solution)/shard_map/ppermute | solution.py:244
  62.7 4.5 %all-to-all-start.2 = ((f32[32,1,640]{2,1,0:T(1,128)}), f32[32,1,640]{2,1,0:T(1,128)S(1)}, u32[]{:S(2)}, u32[]{:S(2)}) async-start(f32[32,1,640]{2,1,0:T(1,128)} %get-tuple-element.73), calls=%async_computation.2 | async-start | bytes 163840 | tf_op jit(solution)/shard_map/all_to_all | solution.py:260
  67.3 1.8 %collective-permute-start.6 = (bf16[256,512]{1,0:T(8,128)(2,1)S(1)}, bf16[256,512]{1,0:T(8,128)(2,1)S(1)}, u32[]{:S(2)}, u32[]{:S(2)}) collective-permute-start(bf16[256,512]{1,0:T(8,128)(2,1)S(1)} %get-tuple-element.71.refs_0_), channel_id=1, source_target_pairs={{0,1},{1,0},{2,3},{3,2},{4,5},{5,4},{6,7},{7,6},{8,9},{9,8},{10,11... | collective-permute-start | bytes 786440 | tf_op jit(solution)/shard_map/ppermute | solution.py:244
  69.1 9.8 %all-to-all-done.2.refs_4_ = f32[32,1,640]{2,1,0:T(1,128)S(1)} async-done(((f32[32,1,640]{2,1,0:T(1,128)}), f32[32,1,640]{2,1,0:T(1,128)S(1)}, u32[]{:S(2)}, u32[]{:S(2)}) %all-to-all-start.2) | async-done | bytes 81952 | tf_op jit(solution)/shard_map/all_to_all | solution.py:260
  80.6 5.0 %mid.5 = (f32[256,512]{1,0:T(8,128)S(1)}, f32[4,512]{1,0:T(4,128)S(1)}, f32[8,128]{1,0:T(8,128)S(1)}, bf16[4,512,512]{2,1,0:T(8,128)(2,1)S(1)}) custom-call(s32[1]{0:T(128)} %bitcast.2.me_ref, bf16[256,512]{1,0:T(8,128)(2,1)S(1)} %get-tuple-element.71.refs_0_, bf16[256,512]{1,0:T(8,128)(2,1)S(1)} %collective-permute-done.6.refs_1_, ...), custom_call_target="tpu_custom_call" | custom-call | flops 536870912 | bytes 10334212 | tf_op jit(solution)/shard_map/mid/pallas_call | solution.py:27
  88.1 2.3 %collective-permute-start.10 = (bf16[256,512]{1,0:T(8,128)(2,1)S(1)}, bf16[256,512]{1,0:T(8,128)(2,1)S(1)}, u32[]{:S(2)}, u32[]{:S(2)}) collective-permute-start(bf16[256,512]{1,0:T(8,128)(2,1)S(1)} %get-tuple-element.80.refs_0_), channel_id=1, source_target_pairs={{0,2},{1,3},{2,0},{3,1},{4,6},{5,7},{6,4},{7,5},{8,10},{9,11},{10,... | collective-permute-start | bytes 786440 | tf_op jit(solution)/shard_map/ppermute | solution.py:244
  90.4 4.5 %all-to-all-start.3 = ((f32[32,1,640]{2,1,0:T(1,128)}), f32[32,1,640]{2,1,0:T(1,128)S(1)}, u32[]{:S(2)}, u32[]{:S(2)}) async-start(f32[32,1,640]{2,1,0:T(1,128)} %get-tuple-element.82), calls=%async_computation.3 | async-start | bytes 163840 | tf_op jit(solution)/shard_map/all_to_all | solution.py:260
  95.0 1.8 %collective-permute-start.9 = (bf16[256,512]{1,0:T(8,128)(2,1)S(1)}, bf16[256,512]{1,0:T(8,128)(2,1)S(1)}, u32[]{:S(2)}, u32[]{:S(2)}) collective-permute-start(bf16[256,512]{1,0:T(8,128)(2,1)S(1)} %get-tuple-element.80.refs_0_), channel_id=1, source_target_pairs={{0,1},{1,0},{2,3},{3,2},{4,5},{5,4},{6,7},{7,6},{8,9},{9,8},{10,11... | collective-permute-start | bytes 786440 | tf_op jit(solution)/shard_map/ppermute | solution.py:244
  96.8 9.3 %all-to-all-done.3.refs_4_ = f32[32,1,640]{2,1,0:T(1,128)S(1)} async-done(((f32[32,1,640]{2,1,0:T(1,128)}), f32[32,1,640]{2,1,0:T(1,128)S(1)}, u32[]{:S(2)}, u32[]{:S(2)}) %all-to-all-start.3) | async-done | bytes 81952 | tf_op jit(solution)/shard_map/all_to_all | solution.py:260
  106.7 1.6 %collective-permute-done.9.refs_1_ = bf16[256,512]{1,0:T(8,128)(2,1)S(1)} collective-permute-done((bf16[256,512]{1,0:T(8,128)(2,1)S(1)}, bf16[256,512]{1,0:T(8,128)(2,1)S(1)}, u32[]{:S(2)}, u32[]{:S(2)}) %collective-permute-start.9) | collective-permute-done | bytes 262176 | tf_op jit(solution)/shard_map/ppermute | solution.py:244
  108.4 5.0 %mid.6 = (f32[256,512]{1,0:T(8,128)S(1)}, f32[4,512]{1,0:T(4,128)S(1)}, f32[8,128]{1,0:T(8,128)S(1)}, bf16[4,512,512]{2,1,0:T(8,128)(2,1)S(1)}) custom-call(s32[1]{0:T(128)} %bitcast.2.me_ref, bf16[256,512]{1,0:T(8,128)(2,1)S(1)} %get-tuple-element.80.refs_0_, bf16[256,512]{1,0:T(8,128)(2,1)S(1)} %collective-permute-done.9.refs_1_, ...), custom_call_target="tpu_custom_call" | custom-call | flops 536870912 | bytes 10334212 | tf_op jit(solution)/shard_map/mid/pallas_call | solution.py:27
  115.4 2.7 %collective-permute-start.13 = (bf16[256,512]{1,0:T(8,128)(2,1)S(1)}, bf16[256,512]{1,0:T(8,128)(2,1)S(1)}, u32[]{:S(2)}, u32[]{:S(2)}) collective-permute-start(bf16[256,512]{1,0:T(8,128)(2,1)S(1)} %get-tuple-element.89.refs_0_), channel_id=1, source_target_pairs={{0,2},{1,3},{2,0},{3,1},{4,6},{5,7},{6,4},{7,5},{8,10},{9,11},{10,... | collective-permute-start | bytes 786440 | tf_op jit(solution)/shard_map/ppermute | solution.py:244
  118.1 4.7 %all-to-all-start.4 = ((f32[32,1,640]{2,1,0:T(1,128)}), f32[32,1,640]{2,1,0:T(1,128)S(1)}, u32[]{:S(2)}, u32[]{:S(2)}) async-start(f32[32,1,640]{2,1,0:T(1,128)} %get-tuple-element.91), calls=%async_computation.4 | async-start | bytes 163840 | tf_op jit(solution)/shard_map/all_to_all | solution.py:260
  122.8 1.7 %collective-permute-start.12 = (bf16[256,512]{1,0:T(8,128)(2,1)S(1)}, bf16[256,512]{1,0:T(8,128)(2,1)S(1)}, u32[]{:S(2)}, u32[]{:S(2)}) collective-permute-start(bf16[256,512]{1,0:T(8,128)(2,1)S(1)} %get-tuple-element.89.refs_0_), channel_id=1, source_target_pairs={{0,1},{1,0},{2,3},{3,2},{4,5},{5,4},{6,7},{7,6},{8,9},{9,8},{10,11... | collective-permute-start | bytes 786440 | tf_op jit(solution)/shard_map/ppermute | solution.py:244
  124.4 9.0 %all-to-all-done.4.refs_4_ = f32[32,1,640]{2,1,0:T(1,128)S(1)} async-done(((f32[32,1,640]{2,1,0:T(1,128)}), f32[32,1,640]{2,1,0:T(1,128)S(1)}, u32[]{:S(2)}, u32[]{:S(2)}) %all-to-all-start.4) | async-done | bytes 81952 | tf_op jit(solution)/shard_map/all_to_all | solution.py:260
  134.1 2.2 %collective-permute-done.12.refs_1_ = bf16[256,512]{1,0:T(8,128)(2,1)S(1)} collective-permute-done((bf16[256,512]{1,0:T(8,128)(2,1)S(1)}, bf16[256,512]{1,0:T(8,128)(2,1)S(1)}, u32[]{:S(2)}, u32[]{:S(2)}) %collective-permute-start.12) | collective-permute-done | bytes 262176 | tf_op jit(solution)/shard_map/ppermute | solution.py:244
  136.3 5.0 %mid.7 = (f32[256,512]{1,0:T(8,128)S(1)}, f32[4,512]{1,0:T(4,128)S(1)}, f32[8,128]{1,0:T(8,128)S(1)}, bf16[4,512,512]{2,1,0:T(8,128)(2,1)S(1)}) custom-call(s32[1]{0:T(128)} %bitcast.2.me_ref, bf16[256,512]{1,0:T(8,128)(2,1)S(1)} %get-tuple-element.89.refs_0_, bf16[256,512]{1,0:T(8,128)(2,1)S(1)} %collective-permute-done.12.refs_1_, ...), custom_call_target="tpu_custom_call" | custom-call | flops 536870912 | bytes 10334212 | tf_op jit(solution)/shard_map/mid/pallas_call | solution.py:27
  143.0 6.6 %all-to-all-start.5 = ((f32[32,1,640]{2,1,0:T(1,128)}), f32[32,1,640]{2,1,0:T(1,128)S(1)}, u32[]{:S(2)}, u32[]{:S(2)}) async-start(f32[32,1,640]{2,1,0:T(1,128)} %get-tuple-element.99), calls=%async_computation.5 | async-start | bytes 163840 | tf_op jit(solution)/shard_map/all_to_all | solution.py:260
  150.9 6.4 %all-to-all-done.5.received_ref = f32[32,1,640]{2,1,0:T(1,128)S(1)} async-done(((f32[32,1,640]{2,1,0:T(1,128)}), f32[32,1,640]{2,1,0:T(1,128)S(1)}, u32[]{:S(2)}, u32[]{:S(2)}) %all-to-all-start.5) | async-done | bytes 81952 | tf_op jit(solution)/shard_map/all_to_all | solution.py:260
  (31 shorter events, 19.4 us)
Async XLA Ops:
  2.4 20.6 %collective-permute-start.1 = (bf16[256,512]{1,0:T(8,128)(2,1)S(1)}, bf16[256,512]{1,0:T(8,128)(2,1)S(1)}, u32[]{:S(2)}, u32[]{:S(2)}) collective-permute-start(bf16[256,512]{1,0:T(8,128)(2,1)S(1)} %get-tuple-element.56.refs_0_), channel_id=1, source_target_pairs={{0,2},{1,3},{2,0},{3,1},{4,6},{5,7},{6,4},{7,5},{8,10},{9,11},{10,... | collective-permute-start | bytes 786440 | tf_op jit(solution)/shard_map/ppermute | solution.py:244
  8.0 15.1 %all-to-all-start = ((f32[32,1,1024]{2,1,0:T(1,128)}), f32[32,1,1024]{2,1,0:T(1,128)S(1)}, u32[]{:S(2)}, u32[]{:S(2)}) async-start(f32[32,1,1024]{2,1,0:T(1,128)} %broadcast_in_dim.11), calls=%async_computation | async-start | bytes 262144 | tf_op jit(solution)/shard_map/all_to_all | solution.py:260
  11.8 14.4 %collective-permute-start = (bf16[256,512]{1,0:T(8,128)(2,1)S(1)}, bf16[256,512]{1,0:T(8,128)(2,1)S(1)}, u32[]{:S(2)}, u32[]{:S(2)}) collective-permute-start(bf16[256,512]{1,0:T(8,128)(2,1)S(1)} %get-tuple-element.56.refs_0_), channel_id=1, source_target_pairs={{0,1},{1,0},{2,3},{3,2},{4,5},{5,4},{6,7},{7,6},{8,9},{9,8},{10,11... | collective-permute-start | bytes 786440 | tf_op jit(solution)/shard_map/ppermute | solution.py:244
  23.0 8.8 %collective-permute-start.2 = (bf16[256,512]{1,0:T(8,128)(2,1)S(1)}, bf16[256,512]{1,0:T(8,128)(2,1)S(1)}, u32[]{:S(2)}, u32[]{:S(2)}) collective-permute-start(bf16[256,512]{1,0:T(8,128)(2,1)S(1)} %collective-permute-done.1.refs_2_), channel_id=1, source_target_pairs={{0,1},{1,0},{2,3},{3,2},{4,5},{5,4},{6,7},{7,6},{8,9},{9,8},{10,11... | collective-permute-start | bytes 786440 | tf_op jit(solution)/shard_map/ppermute | solution.py:244
  33.2 18.4 %collective-permute-start.4 = (bf16[256,512]{1,0:T(8,128)(2,1)S(1)}, bf16[256,512]{1,0:T(8,128)(2,1)S(1)}, u32[]{:S(2)}, u32[]{:S(2)}) collective-permute-start(bf16[256,512]{1,0:T(8,128)(2,1)S(1)} %get-tuple-element.62.refs_0_), channel_id=1, source_target_pairs={{0,2},{1,3},{2,0},{3,1},{4,6},{5,7},{6,4},{7,5},{8,10},{9,11},{10,... | collective-permute-start | bytes 786440 | tf_op jit(solution)/shard_map/ppermute | solution.py:244
  35.2 16.4 %all-to-all-start.1 = ((f32[32,1,640]{2,1,0:T(1,128)}), f32[32,1,640]{2,1,0:T(1,128)S(1)}, u32[]{:S(2)}, u32[]{:S(2)}) async-start(f32[32,1,640]{2,1,0:T(1,128)} %get-tuple-element.64), calls=%async_computation.1 | async-start | bytes 163840 | tf_op jit(solution)/shard_map/all_to_all | solution.py:260
  39.6 14.1 %collective-permute-start.3 = (bf16[256,512]{1,0:T(8,128)(2,1)S(1)}, bf16[256,512]{1,0:T(8,128)(2,1)S(1)}, u32[]{:S(2)}, u32[]{:S(2)}) collective-permute-start(bf16[256,512]{1,0:T(8,128)(2,1)S(1)} %get-tuple-element.62.refs_0_), channel_id=1, source_target_pairs={{0,1},{1,0},{2,3},{3,2},{4,5},{5,4},{6,7},{7,6},{8,9},{9,8},{10,11... | collective-permute-start | bytes 786440 | tf_op jit(solution)/shard_map/ppermute | solution.py:244
  51.6 7.8 %collective-permute-start.5 = (bf16[256,512]{1,0:T(8,128)(2,1)S(1)}, bf16[256,512]{1,0:T(8,128)(2,1)S(1)}, u32[]{:S(2)}, u32[]{:S(2)}) collective-permute-start(bf16[256,512]{1,0:T(8,128)(2,1)S(1)} %collective-permute-done.4.refs_2_), channel_id=1, source_target_pairs={{0,1},{1,0},{2,3},{3,2},{4,5},{5,4},{6,7},{7,6},{8,9},{9,8},{10,11... | collective-permute-start | bytes 786440 | tf_op jit(solution)/shard_map/ppermute | solution.py:244
  60.8 18.1 %collective-permute-start.7 = (bf16[256,512]{1,0:T(8,128)(2,1)S(1)}, bf16[256,512]{1,0:T(8,128)(2,1)S(1)}, u32[]{:S(2)}, u32[]{:S(2)}) collective-permute-start(bf16[256,512]{1,0:T(8,128)(2,1)S(1)} %get-tuple-element.71.refs_0_), channel_id=1, source_target_pairs={{0,2},{1,3},{2,0},{3,1},{4,6},{5,7},{6,4},{7,5},{8,10},{9,11},{10,... | collective-permute-start | bytes 786440 | tf_op jit(solution)/shard_map/ppermute | solution.py:244
  62.7 16.2 %all-to-all-start.2 = ((f32[32,1,640]{2,1,0:T(1,128)}), f32[32,1,640]{2,1,0:T(1,128)S(1)}, u32[]{:S(2)}, u32[]{:S(2)}) async-start(f32[32,1,640]{2,1,0:T(1,128)} %get-tuple-element.73), calls=%async_computation.2 | async-start | bytes 163840 | tf_op jit(solution)/shard_map/all_to_all | solution.py:260
  67.3 13.4 %collective-permute-start.6 = (bf16[256,512]{1,0:T(8,128)(2,1)S(1)}, bf16[256,512]{1,0:T(8,128)(2,1)S(1)}, u32[]{:S(2)}, u32[]{:S(2)}) collective-permute-start(bf16[256,512]{1,0:T(8,128)(2,1)S(1)} %get-tuple-element.71.refs_0_), channel_id=1, source_target_pairs={{0,1},{1,0},{2,3},{3,2},{4,5},{5,4},{6,7},{7,6},{8,9},{9,8},{10,11... | collective-permute-start | bytes 786440 | tf_op jit(solution)/shard_map/ppermute | solution.py:244
  78.9 7.8 %collective-permute-start.8 = (bf16[256,512]{1,0:T(8,128)(2,1)S(1)}, bf16[256,512]{1,0:T(8,128)(2,1)S(1)}, u32[]{:S(2)}, u32[]{:S(2)}) collective-permute-start(bf16[256,512]{1,0:T(8,128)(2,1)S(1)} %collective-permute-done.7.refs_2_), channel_id=1, source_target_pairs={{0,1},{1,0},{2,3},{3,2},{4,5},{5,4},{6,7},{7,6},{8,9},{9,8},{10,11... | collective-permute-start | bytes 786440 | tf_op jit(solution)/shard_map/ppermute | solution.py:244
  88.1 18.0 %collective-permute-start.10 = (bf16[256,512]{1,0:T(8,128)(2,1)S(1)}, bf16[256,512]{1,0:T(8,128)(2,1)S(1)}, u32[]{:S(2)}, u32[]{:S(2)}) collective-permute-start(bf16[256,512]{1,0:T(8,128)(2,1)S(1)} %get-tuple-element.80.refs_0_), channel_id=1, source_target_pairs={{0,2},{1,3},{2,0},{3,1},{4,6},{5,7},{6,4},{7,5},{8,10},{9,11},{10,... | collective-permute-start | bytes 786440 | tf_op jit(solution)/shard_map/ppermute | solution.py:244
  90.4 15.7 %all-to-all-start.3 = ((f32[32,1,640]{2,1,0:T(1,128)}), f32[32,1,640]{2,1,0:T(1,128)S(1)}, u32[]{:S(2)}, u32[]{:S(2)}) async-start(f32[32,1,640]{2,1,0:T(1,128)} %get-tuple-element.82), calls=%async_computation.3 | async-start | bytes 163840 | tf_op jit(solution)/shard_map/all_to_all | solution.py:260
  95.0 13.4 %collective-permute-start.9 = (bf16[256,512]{1,0:T(8,128)(2,1)S(1)}, bf16[256,512]{1,0:T(8,128)(2,1)S(1)}, u32[]{:S(2)}, u32[]{:S(2)}) collective-permute-start(bf16[256,512]{1,0:T(8,128)(2,1)S(1)} %get-tuple-element.80.refs_0_), channel_id=1, source_target_pairs={{0,1},{1,0},{2,3},{3,2},{4,5},{5,4},{6,7},{7,6},{8,9},{9,8},{10,11... | collective-permute-start | bytes 786440 | tf_op jit(solution)/shard_map/ppermute | solution.py:244
  106.1 7.8 %collective-permute-start.11 = (bf16[256,512]{1,0:T(8,128)(2,1)S(1)}, bf16[256,512]{1,0:T(8,128)(2,1)S(1)}, u32[]{:S(2)}, u32[]{:S(2)}) collective-permute-start(bf16[256,512]{1,0:T(8,128)(2,1)S(1)} %collective-permute-done.10.refs_2_), channel_id=1, source_target_pairs={{0,1},{1,0},{2,3},{3,2},{4,5},{5,4},{6,7},{7,6},{8,9},{9,8},{10,11... | collective-permute-start | bytes 786440 | tf_op jit(solution)/shard_map/ppermute | solution.py:244
  115.4 18.1 %collective-permute-start.13 = (bf16[256,512]{1,0:T(8,128)(2,1)S(1)}, bf16[256,512]{1,0:T(8,128)(2,1)S(1)}, u32[]{:S(2)}, u32[]{:S(2)}) collective-permute-start(bf16[256,512]{1,0:T(8,128)(2,1)S(1)} %get-tuple-element.89.refs_0_), channel_id=1, source_target_pairs={{0,2},{1,3},{2,0},{3,1},{4,6},{5,7},{6,4},{7,5},{8,10},{9,11},{10,... | collective-permute-start | bytes 786440 | tf_op jit(solution)/shard_map/ppermute | solution.py:244
  118.1 15.4 %all-to-all-start.4 = ((f32[32,1,640]{2,1,0:T(1,128)}), f32[32,1,640]{2,1,0:T(1,128)S(1)}, u32[]{:S(2)}, u32[]{:S(2)}) async-start(f32[32,1,640]{2,1,0:T(1,128)} %get-tuple-element.91), calls=%async_computation.4 | async-start | bytes 163840 | tf_op jit(solution)/shard_map/all_to_all | solution.py:260
  122.8 13.5 %collective-permute-start.12 = (bf16[256,512]{1,0:T(8,128)(2,1)S(1)}, bf16[256,512]{1,0:T(8,128)(2,1)S(1)}, u32[]{:S(2)}, u32[]{:S(2)}) collective-permute-start(bf16[256,512]{1,0:T(8,128)(2,1)S(1)} %get-tuple-element.89.refs_0_), channel_id=1, source_target_pairs={{0,1},{1,0},{2,3},{3,2},{4,5},{5,4},{6,7},{7,6},{8,9},{9,8},{10,11... | collective-permute-start | bytes 786440 | tf_op jit(solution)/shard_map/ppermute | solution.py:244
  133.5 8.1 %collective-permute-start.14 = (bf16[256,512]{1,0:T(8,128)(2,1)S(1)}, bf16[256,512]{1,0:T(8,128)(2,1)S(1)}, u32[]{:S(2)}, u32[]{:S(2)}) collective-permute-start(bf16[256,512]{1,0:T(8,128)(2,1)S(1)} %collective-permute-done.13.refs_2_), channel_id=1, source_target_pairs={{0,1},{1,0},{2,3},{3,2},{4,5},{5,4},{6,7},{7,6},{8,9},{9,8},{10,11... | collective-permute-start | bytes 786440 | tf_op jit(solution)/shard_map/ppermute | solution.py:244
  143.0 14.2 %all-to-all-start.5 = ((f32[32,1,640]{2,1,0:T(1,128)}), f32[32,1,640]{2,1,0:T(1,128)S(1)}, u32[]{:S(2)}, u32[]{:S(2)}) async-start(f32[32,1,640]{2,1,0:T(1,128)} %get-tuple-element.99), calls=%async_computation.5 | async-start | bytes 163840 | tf_op jit(solution)/shard_map/all_to_all | solution.py:260
